TPU v7x, 512 devices: a whole 4x4x16 slice. The times are simulated.
512 devices in a mesh: row: 32 (over z_hi, x, core), col: 16 (over y, z_lo).
Axes of the slice: x: 4, y: 4, z: 16 (z_hi: 4, z_lo: 4; z = z_hi * 4 + z_lo), core: 2. Of those that a mesh axis runs over, the one named last changes fastest.
Arguments:
- right_sides: float32 [8, 131072], P(None, ('row', 'col')), may hold values from -11 to 11
- noise_var: float32 [131072], P(('row', 'col')), may hold values from 1.2 to 3
- observed: int32 [131072], P(('row', 'col')), may hold values 0 or 1
- tile_data: bfloat16 [32, 16, 32, 128, 128], P('row', 'col'), may hold values from -1 to 1
- diag_tiles: bfloat16 [1024, 128, 128], P(('row', 'col')), may hold values from -1 to 1
- tile_rows: int32 [32, 16, 32], P('row', 'col'), may hold values from 0 to 63
- tile_cols: int32 [32, 16, 32], P('row', 'col'), may hold values from 0 to 31
- tile_count: int32 [32, 16], P('row', 'col'), may hold values from 16 to 32, as said below
Outputs:
- solution: float32 [8, 131072], P(None, ('row', 'col'))
- residual: float32 [8, 131072], P(None, ('row', 'col'))
Inputs may be any that keep to these rules, and one draw needn't show every extreme that they name: A device's slots t < tile_count name distinct pairs (i, j) whose blocks satisfy I != J, with I < J exactly when I + J is even, so that each pair of blocks is stored at most once; slots beyond the count hold arbitrary indices in range. Every device of the last row has exactly 32 live slots.
All inputs are finite; a program needn't handle non-finite values. No bound on the sum of `observed` on one device may be relied on, other than what follows from the above.
Results may differ from a plain program's by a relative error of at most 0.0003.
Values sent between devices are 32-bit elements; how exact they have to be, the bound alone decides.
A program may use at most 64 MiB of HBM per device.

v0:
```python
import math

import jax
import jax.numpy as jnp
from jax import lax
from jax.sharding import PartitionSpec as P

TILE = 128
COUPLED = 32
ITERS = 2


def residual_norms(residual):
    return lax.psum(jnp.sum(residual * residual, axis=1), ("row", "col"))


def local(
    right_sides, noise_var, observed, tile_data, diag_tiles, tile_rows, tile_cols, tile_count
):
    rhs_count = right_sides.shape[0]
    block_here = diag_tiles.shape[0]
    tile_size = diag_tiles.shape[1]
    piece_len = block_here * tile_size
    row_devices = lax.axis_size("row")
    col_devices = lax.axis_size("col")
    coupling = 1.0 / (2.0 * math.sqrt(TILE * (2 * COUPLED + 1)))
    highest = lax.Precision.HIGHEST
    observed_float = observed.astype(jnp.float32)[None, :]
    noise_row = noise_var[None, :]
    local_tiles = tile_data[0, 0].astype(jnp.float32)
    picks_row = tile_rows[0, 0]
    picks_col = tile_cols[0, 0]
    live_slots = jnp.arange(local_tiles.shape[0]) < tile_count[0, 0]
    row_hot = (
        (picks_row[:, None] == jnp.arange(row_devices * block_here)[None, :]) & live_slots[:, None]
    ).astype(jnp.float32)
    col_hot = (
        (picks_col[:, None] == jnp.arange(col_devices * block_here)[None, :]) & live_slots[:, None]
    ).astype(jnp.float32)
    row_index = jnp.arange(tile_size)[:, None]
    col_index = jnp.arange(tile_size)[None, :]
    diag_float = diag_tiles.astype(jnp.float32)
    zero_tiles = jnp.zeros_like(diag_float)
    diag_upper = jnp.where((col_index >= row_index)[None, :, :], diag_float, zero_tiles)
    diag_strict = jnp.where((col_index > row_index)[None, :, :], diag_float, zero_tiles)
    solution = jnp.zeros_like(right_sides)
    residual = right_sides
    direction = right_sides
    norm_now = residual_norms(residual)
    for iteration in range(ITERS):
        masked = observed_float * direction
        by_col = lax.all_gather(masked, "col", axis=1, tiled=True)
        by_row = lax.all_gather(masked, "row", axis=1, tiled=True)
        by_col = by_col.reshape(rhs_count, col_devices * block_here, tile_size)
        by_row = by_row.reshape(rhs_count, row_devices * block_here, tile_size)
        upper_terms = jnp.einsum(
            "tab,stb->sta", local_tiles, jnp.take(by_col, picks_col, axis=1), precision=highest
        )
        row_terms = jnp.einsum("sta,ti->sia", upper_terms, row_hot, precision=highest)
        own_rows = lax.psum_scatter(
            row_terms.reshape(rhs_count, row_devices * piece_len),
            "row",
            scatter_dimension=1,
            tiled=True,
        )
        lower_terms = jnp.einsum(
            "tab,sta->stb", local_tiles, jnp.take(by_row, picks_row, axis=1), precision=highest
        )
        col_terms = jnp.einsum("stb,tj->sjb", lower_terms, col_hot, precision=highest)
        mirrored = lax.psum_scatter(
            col_terms.reshape(rhs_count, col_devices * piece_len),
            "col",
            scatter_dimension=1,
            tiled=True,
        )
        local_blocks = masked.reshape(rhs_count, block_here, tile_size)
        diag_terms = jnp.einsum("kab,skb->ska", diag_upper, local_blocks, precision=highest)
        diag_terms = diag_terms + jnp.einsum(
            "kab,ska->skb", diag_strict, local_blocks, precision=highest
        )
        total = own_rows + mirrored + diag_terms.reshape(rhs_count, piece_len)
        image_field = noise_row * direction + observed_float * (coupling * total)
        step_alpha = norm_now / lax.psum(jnp.sum(direction * image_field, axis=1), ("row", "col"))
        solution = solution + step_alpha[:, None] * direction
        residual = residual - step_alpha[:, None] * image_field
        norm_next = residual_norms(residual)
        direction = residual + (norm_next / norm_now)[:, None] * direction
        norm_now = norm_next
    return (solution, residual)


def solution(mesh):
    return jax.shard_map(
        local,
        mesh=mesh,
        in_specs=(
            P(None, ("row", "col")),
            P(("row", "col")),
            P(("row", "col")),
            P("row", "col", None, None, None),
            P(("row", "col"), None, None),
            P("row", "col", None),
            P("row", "col", None),
            P("row", "col"),
        ),
        out_specs=(P(None, ("row", "col")), P(None, ("row", "col"))),
        check_vma=False,
    )
```

profile of v0, /device:TPU:1, one launch (start us, length us, event | category | flops | bytes accessed | tf_op | source)
XLA Modules:
  0.0 862.3 jit_solution(10460393890309216565)
XLA Ops:
  7.2 0.0 copy-start
  7.2 0.0 reduce-scatter.7.cloned.1.call-start
  7.2 0.7 compare_select_fusion
  8.0 0.7 convert_element_type.4
  9.4 61.0 %all_gather.13 = f32[8,8192]{1,0:T(8,128)S(1)} all-gather(f32[8,256]{1,0:T(8,128)S(1)} %broadcast_multiply_fusion.1), channel_id=1, replica_groups=mesh['row'=32,'col'=16] {'row'}, dimensions={1}, use_global_device_ids=true | all-gather | bytes 270336 | tf_op jit(solution)/shard_map/all_gather | solution.py:53
  70.4 0.6 gather_fusion.1
  71.0 1.0 fusion.12
  72.0 0.7 copy-done.3
  72.7 0.2 convolution_bitcast_fusion.3
  72.9 0.7 copy.41
  73.6 0.0 reduce-scatter.7.cloned.1.call-update
  73.6 0.0 reduce-scatter.5.cloned.1.call-start
  73.7 35.8 %all_gather.12 = f32[8,4096]{1,0:T(8,128)S(1)} all-gather(f32[8,256]{1,0:T(8,128)S(1)} %broadcast_multiply_fusion.1), channel_id=1, replica_groups=mesh['row'=32,'col'=16] {'col'}, dimensions={1}, use_global_device_ids=true | all-gather | bytes 139264 | tf_op jit(solution)/shard_map/all_gather | solution.py:52
  109.5 0.6 gather_fusion
  110.1 1.8 fusion.14
  111.8 0.4 convolution_bitcast_fusion.1
  112.2 0.8 copy.39
  113.1 0.0 reduce-scatter.5.cloned.1.call-update
  113.1 0.0 reduce-scatter.11.cloned.1.call-start
  113.2 0.6 copy-done.2
  113.8 0.1 copy-done.5
  114.0 0.3 fusion.17
  114.2 28.7 %reduce-scatter.7.cloned.1.call-done = f32[8,256]{1,0:T(8,128)} async-done(((f32[8,4096]{1,0:T(8,128)}), f32[8,256]{1,0:T(8,128)}) %reduce-scatter.7.cloned.1.call-update) | async-done | bytes 8208 | tf_op jit(solution)/shard_map/reduce_scatter | solution.py:70
  143.0 121.6 %reduce-scatter.5.cloned.1.call-done = f32[8,256]{1,0:T(8,128)} async-done(((f32[8,8192]{1,0:T(8,128)}), f32[8,256]{1,0:T(8,128)}) %reduce-scatter.5.cloned.1.call-update) | async-done | bytes 8208 | tf_op jit(solution)/shard_map/reduce_scatter | solution.py:60
  264.6 1.1 multiply_reduce_fusion.2
  265.7 101.8 %all-reduce = (f32[8]{0:T(128)S(1)}, f32[8]{0:T(128)S(1)}) all-reduce(f32[8]{0:T(128)S(1)} %get-tuple-element.5, f32[8]{0:T(128)S(1)} %get-tuple-element.4), channel_id=1, replica_groups=mesh['row'=32,'col'=16] {'row','col'}, use_global_device_ids=true, to_apply=%region_1.2 | all-reduce | flops 16 | bytes 128 | tf_op jit(solution)/shard_map/psum | solution.py:14
  367.4 0.2 multiply_reduce_fusion.1
  367.6 100.1 %psum.30 = f32[8]{0:T(128)S(1)} all-reduce(f32[8]{0:T(128)S(1)} %multiply_reduce_fusion.1), channel_id=1, replica_groups=mesh['row'=32,'col'=16] {'row','col'}, use_global_device_ids=true, to_apply=%region_7.10 | all-reduce | flops 8 | bytes 64 | tf_op jit(solution)/shard_map/psum | solution.py:14
  467.8 0.1 broadcast_multiply_fusion
  467.9 34.1 %all_gather.14 = f32[8,4096]{1,0:T(8,128)S(1)} all-gather(f32[8,256]{1,0:T(8,128)S(1)} %get-tuple-element.8), channel_id=1, replica_groups=mesh['row'=32,'col'=16] {'col'}, dimensions={1}, use_global_device_ids=true | all-gather | bytes 139264 | tf_op jit(solution)/shard_map/all_gather | solution.py:52
  502.0 57.3 %all_gather.15 = f32[8,8192]{1,0:T(8,128)S(1)} all-gather(f32[8,256]{1,0:T(8,128)S(1)} %get-tuple-element.8), channel_id=1, replica_groups=mesh['row'=32,'col'=16] {'row'}, dimensions={1}, use_global_device_ids=true | all-gather | bytes 270336 | tf_op jit(solution)/shard_map/all_gather | solution.py:53
  559.3 0.6 gather_fusion.2
  559.9 0.6 gather_fusion.3
  560.5 1.0 fusion.8
  561.4 0.2 convolution_bitcast_fusion.2
  561.7 0.7 copy.40
  562.4 0.0 reduce-scatter.11.cloned.1.call-update
  562.4 0.0 reduce-scatter.9.cloned.1.call-start
  562.5 1.8 fusion.10
  564.2 0.4 convolution_bitcast_fusion
  564.6 0.8 copy.38
  565.5 0.0 reduce-scatter.9.cloned.1.call-update
  565.5 0.3 fusion.16
  565.8 64.8 %reduce-scatter.11.cloned.1.call-done = f32[8,256]{1,0:T(8,128)} async-done(((f32[8,4096]{1,0:T(8,128)}), f32[8,256]{1,0:T(8,128)}) %reduce-scatter.11.cloned.1.call-update) | async-done | bytes 8208 | tf_op jit(solution)/shard_map/reduce_scatter | solution.py:70
  630.7 121.7 %reduce-scatter.9.cloned.1.call-done = f32[8,256]{1,0:T(8,128)} async-done(((f32[8,8192]{1,0:T(8,128)}), f32[8,256]{1,0:T(8,128)}) %reduce-scatter.9.cloned.1.call-update) | async-done | bytes 8208 | tf_op jit(solution)/shard_map/reduce_scatter | solution.py:60
  752.3 1.0 multiply_reduce_fusion
  753.4 101.7 %psum.31 = f32[8]{0:T(128)S(1)} all-reduce(f32[8]{0:T(128)S(1)} %get-tuple-element.13), channel_id=1, replica_groups=mesh['row'=32,'col'=16] {'row','col'}, use_global_device_ids=true, to_apply=%region_11.14 | all-reduce | flops 8 | bytes 64 | tf_op jit(solution)/shard_map/psum | solution.py:83
  855.1 0.7 multiply_subtract_fusion
  (23 shorter events, 0.1 us)
Async XLA Ops:
  7.2 63.8 %copy-start = (bf16[1,1,32,128,128]{4,3,2,1,0:T(8,128)(2,1)S(1)}, bf16[1,1,32,128,128]{4,3,2,1,0:T(8,128)(2,1)}, u32[]{:S(2)}) copy-start(bf16[1,1,32,128,128]{4,3,2,1,0:T(8,128)(2,1)} %param.15) | copy-start | bytes 3145732
  7.2 0.8 copy-start.4
  7.2 2.2 copy-start.1
  7.2 135.8 %reduce-scatter.7.cloned.1.call-start = ((), (), s32[]{:S(2)}) async-start(), calls=%async_computation.5 | async-start | bytes 139264 | tf_op jit(solution)/shard_map/reduce_scatter | solution.py:70
  72.0 0.7 copy-start.3
  73.6 191.0 %reduce-scatter.5.cloned.1.call-start = ((), (), s32[]{:S(2)}) async-start(), calls=%async_computation.4 | async-start | bytes 270336 | tf_op jit(solution)/shard_map/reduce_scatter | solution.py:60
  113.1 0.7 copy-start.2
  113.1 0.9 copy-start.5
  113.1 517.5 %reduce-scatter.11.cloned.1.call-start = ((), (), s32[]{:S(2)}) async-start(), calls=%async_computation.7 | async-start | bytes 139264 | tf_op jit(solution)/shard_map/reduce_scatter | solution.py:70
  114.0 150.6 %copy-start.6 = (f32[256]{0:T(256)S(1)}, f32[256]{0:T(256)}, u32[]{:S(2)}) copy-start(f32[256]{0:T(256)} %param.13) | copy-start | bytes 3076
  562.4 189.9 %reduce-scatter.9.cloned.1.call-start = ((), (), s32[]{:S(2)}) async-start(), calls=%async_computation.6 | async-start | bytes 270336 | tf_op jit(solution)/shard_map/reduce_scatter | solution.py:60
Sparse Core Ops, SparseCore 0:
  73.7 69.1 reduce-scatter.6
  147.3 117.2 reduce-scatter.4
  562.5 68.0 reduce-scatter.10
  634.8 117.4 reduce-scatter.8
where the time goes:
time: 863 us; the launch traced here: 862 us
  blocking collectives  492 us (57%)
  waiting for transfers between devices  337 us (39%)
  between operations  14.6 us (2%)
  matrix products  9.38 us (1%)
    reduce_scatter x2, waiting for transfers between devices, local(): lax.psum_scatter(row_terms.reshape(rhs_count, row_devices * piece_len), '...  243 us
    psum x2, blocking collectives, residual_norms(): return lax.psum(jnp.sum(residual * residual, axis=1), ('row', 'col'))  202 us
    all_gather x2, blocking collectives, local(): by_row = lax.all_gather(masked, 'row', axis=1, tiled=True)  118 us
    psum x1, blocking collectives, local(): lax.psum(jnp.sum(direction * image_field, axis=1), ('row', 'col'))  102 us
    reduce_scatter x2, waiting for transfers between devices, local(): lax.psum_scatter(col_terms.reshape(rhs_count, col_devices * piece_len), '...  93.6 us
    all_gather x2, blocking collectives, local(): by_col = lax.all_gather(masked, 'col', axis=1, tiled=True)  69.9 us
  transfers between devices with their start and end apart: 4, of which 4 were waited for; matrix products, arithmetic and copies ran while one was open for 1% of the time, Pallas kernels for 0%

commit v1 on v0

v1 whole, which is shorter than its diff:
```python
import functools
import math

import jax
import jax.numpy as jnp
from jax import lax
from jax.experimental import pallas as pl
from jax.experimental.pallas import tpu as pltpu
from jax.sharding import PartitionSpec as P

TILE = 128
COUPLED = 32
NRHS = 8
MESH = pl.DeviceIdType.MESH
ROW_PARTS = (4, 4, 2)
COL_PARTS = (4, 4)
F32 = jnp.float32
BF16 = jnp.bfloat16


def split_rows(value):
    high = value.astype(BF16).astype(F32)
    return jnp.concatenate([high, value - high], axis=0).astype(BF16)


def near_first(size):
    return sorted(range(1, size), key=lambda d: min(d, size - d))


def kernel(
    rparts,
    cparts,
    rs_ref,
    noise_ref,
    obs_ref,
    diag_hbm,
    tile_hbm,
    rows_s,
    cols_s,
    count_s,
    sol_ref,
    res_ref,
    tiles,
    diag,
    sym,
    hrow,
    hcol,
    rowbuf,
    colbuf,
    rowsplit,
    colsplit,
    gath,
    rowterm,
    colterm,
    xrecv,
    zsend,
    zrecv,
    yrecv,
    lsend,
    lrecv,
    red_src,
    red_dst,
    local_sem,
    agz_sem,
    agx_sem,
    agl_sem,
    agy_sem,
    rsx_sem,
    rsz_sem,
    rcy_sem,
    rcl_sem,
    red_sem,
):
    nzh, nx, nc = rparts
    ny, nzl = cparts
    nrow, ncol = nzh * nx * nc, ny * nzl
    slots = tile_hbm.shape[0]
    coupling = 1.0 / (2.0 * math.sqrt(TILE * (2 * COUPLED + 1)))

    row = lax.axis_index("row")
    col = lax.axis_index("col")
    zh, x, core = row // (nx * nc), row // nc % nx, row % nc
    y, zl = col // nzl, col % nzl

    def row_at(dz, dx, dc):
        return (
            lax.rem(zh + dz, nzh) * (nx * nc)
            + lax.rem(x + dx, nx) * nc
            + lax.rem(core + dc, nc)
        )

    def col_at(dy, dl):
        return lax.rem(y + dy, ny) * nzl + lax.rem(zl + dl, nzl)

    def row_from(dz, dx, dc):
        return row_at(nzh - dz, nx - dx, nc - dc)

    def col_from(dy, dl):
        return col_at(ny - dy, nzl - dl)

    plane = [(dx, dc) for dx in range(nx) for dc in range(nc) if dx or dc]
    plane = sorted(plane, key=lambda p: -min(p[0], nx - p[0]))
    line = [(dz, dl) for dz in range(nzh) for dl in range(nzl) if dz or dl]
    line = sorted(line, key=lambda p: -min(p[0] * nzl + p[1], nzh * nzl - p[0] * nzl - p[1]))
    zs, ys, ls = near_first(nzh), near_first(ny), list(range(1, nzl))

    barrier = pltpu.get_barrier_semaphore()
    peers = [(row_at(dz, 0, 0), col_at(0, dl)) for dz, dl in line]
    peers += [(row_at(0, dx, dc), col) for dx, dc in plane]
    peers += [(row, col_at(dy, 0)) for dy in ys]
    for peer in peers:
        pl.semaphore_signal(barrier, inc=1, device_id=peer, device_id_type=MESH)

    pending = []

    def remote(src, dst, sems, index, device):
        return pltpu.make_async_remote_copy(
            src_ref=src,
            dst_ref=dst,
            send_sem=sems.at[(0, *index)],
            recv_sem=sems.at[(1, *index)],
            device_id=device,
            device_id_type=MESH,
        )

    def send(src, dst, sems, index, device):
        copy = remote(src, dst, sems, index, device)
        copy.start()
        pending.append(copy)

    def arrive(dst, sems, index):
        remote(dst, dst, sems, index, (row, col)).wait_recv()

    tile_copy = pltpu.make_async_copy(tile_hbm, tiles, local_sem.at[0])
    diag_copy = pltpu.make_async_copy(diag_hbm, diag, local_sem.at[1])
    diag_copy.start()
    tile_copy.start()

    observed = [obs_ref[:, k * TILE : (k + 1) * TILE].astype(F32) for k in range(2)]
    noise = [noise_ref[:, k * TILE : (k + 1) * TILE] for k in range(2)]
    right = [rs_ref[:, k * TILE : (k + 1) * TILE] for k in range(2)]

    def chunk_row(it, r):
        return rowbuf.at[it, pl.ds(2 * r, 2)]

    def chunk_col(it, c):
        return colbuf.at[it, pl.ds(2 * c, 2)]

    def put_masked(it, masked):
        for k in range(2):
            rowbuf[it, 2 * row + k] = masked[k]
            colbuf[it, 2 * col + k] = masked[k]

    def start_gather(it):
        mine_r, mine_c = chunk_row(it, row), chunk_col(it, col)
        for d in reversed(zs):
            send(mine_r, mine_r, agz_sem, (it, d), (row_at(d, 0, 0), col))
        for d in ls:
            send(mine_c, mine_c, agl_sem, (it, d), (row, col_at(0, d)))
        for d in ys:
            send(mine_c, mine_c, agy_sem, (it, 0, d), (row, col_at(d, 0)))
        for dx, dc in plane:
            send(mine_r, mine_r, agx_sem, (it, 0, dx * nc + dc), (row_at(0, dx, dc), col))

    def col_forward(it, d):
        got = chunk_col(it, col_from(0, d))
        arrive(got, agl_sem, (it, d))
        for dy in ys:
            send(got, got, agy_sem, (it, d, dy), (row, col_at(dy, 0)))

    def row_forward(it, d):
        got = chunk_row(it, row_from(d, 0, 0))
        arrive(got, agz_sem, (it, d))
        for dx, dc in plane:
            send(got, got, agx_sem, (it, d, dx * nc + dc), (row_at(0, dx, dc), col))

    def col_done(it):
        for d in range(nzl):
            for dy in ys:
                arrive(chunk_col(it, col_from(dy, d)), agy_sem, (it, d, dy))

    def row_done(it):
        for d in [0, *zs]:
            for dx, dc in plane:
                arrive(
                    chunk_row(it, row_from(d, dx, dc)), agx_sem, (it, d, dx * nc + dc)
                )

    def product(hot, value):
        high = value.astype(BF16)
        low = (value - high.astype(F32)).astype(BF16)
        both = jnp.concatenate([high, low], axis=1)
        sums = jnp.dot(hot, both, preferred_element_type=F32)
        return sums[:, :TILE] + sums[:, TILE:]

    def terms(picks, pieces, contract):
        for t in range(slots):
            gath[t] = pieces[picks[t]]
        out = lax.dot_general(
            gath[...],
            tiles[...],
            (((2,), (contract,)), ((0,), (0,))),
            preferred_element_type=F32,
        )
        return (out[:, :NRHS] + out[:, NRHS:]).reshape(slots * NRHS, TILE)

    def upper(it):
        for j in range(2 * ncol):
            colsplit[j] = split_rows(colbuf[it, j])
        value = terms(cols_s, colsplit, 2)
        rowterm[it] = product(hrow[...], value).reshape(2 * nrow, NRHS, TILE)
        for dz in [*reversed(zs), 0]:
            for dx, dc in plane:
                send(
                    rowterm.at[it, pl.ds(2 * row_at(dz, dx, dc), 2)],
                    xrecv.at[it, dz, dx * nc + dc],
                    rsx_sem,
                    (it, dz, dx * nc + dc),
                    (row_at(0, dx, dc), col),
                )

    def lower(it):
        for i in range(2 * nrow):
            rowsplit[i] = split_rows(rowbuf[it, i])
        value = terms(rows_s, rowsplit, 1)
        colterm[it] = product(hcol[...], value).reshape(2 * ncol, NRHS, TILE)
        for dl in [*ls, 0]:
            for dy in ys:
                send(
                    colterm.at[it, pl.ds(2 * col_at(dy, dl), 2)],
                    yrecv.at[it, dl, dy],
                    rcy_sem,
                    (it, dl, dy),
                    (row, col_at(dy, 0)),
                )

    def row_reduce(it, dz):
        for dx, dc in plane:
            arrive(xrecv.at[it, dz, dx * nc + dc], rsx_sem, (it, dz, dx * nc + dc))
        total = rowterm[it, pl.ds(2 * row_at(dz, 0, 0), 2)]
        for dx, dc in plane:
            total = total + xrecv[it, dz, dx * nc + dc]
        zsend[it, dz] = total
        if dz:
            send(zsend.at[it, dz], zrecv.at[it, dz], rsz_sem, (it, dz), (row_at(dz, 0, 0), col))

    def col_reduce(it, dl):
        for dy in ys:
            arrive(yrecv.at[it, dl, dy], rcy_sem, (it, dl, dy))
        total = colterm[it, pl.ds(2 * col_at(0, dl), 2)]
        for dy in ys:
            total = total + yrecv[it, dl, dy]
        lsend[it, dl] = total
        if dl:
            send(lsend.at[it, dl], lrecv.at[it, dl], rcl_sem, (it, dl), (row, col_at(0, dl)))

    def row_final(it):
        total = zsend[it, 0]
        for d in zs:
            arrive(zrecv.at[it, d], rsz_sem, (it, d))
            total = total + zrecv[it, d]
        return total

    def col_final(it):
        total = lsend[it, 0]
        for d in ls:
            arrive(lrecv.at[it, d], rcl_sem, (it, d))
            total = total + lrecv[it, d]
        return total

    lane = lax.broadcasted_iota(jnp.int32, (NRHS, TILE), 1)
    sub = lax.broadcasted_iota(jnp.int32, (NRHS, TILE), 0)
    stages = (
        [(dx * nc + dc, (row_at(0, dx, dc), col)) for dx, dc in plane],
        [(dy, (row, col_at(dy, 0))) for dy in ys],
        [(dz * nzl + dl, (row_at(dz, 0, 0), col_at(0, dl))) for dz, dl in line],
    )

    def red_send(r, stage, value):
        red_src[r, stage] = value
        for slot, device in stages[stage]:
            send(
                red_src.at[r, stage],
                red_dst.at[r, stage, slot],
                red_sem,
                (r, stage, slot),
                device,
            )

    def red_get(r, stage):
        for slot, _ in stages[stage]:
            arrive(red_dst.at[r, stage, slot], red_sem, (r, stage, slot))
        total = red_src[r, stage]
        for slot, _ in stages[stage]:
            total = total + red_dst[r, stage, slot]
        return total

    def pack(values):
        packed = jnp.zeros((NRHS, TILE), F32)
        for k, value in enumerate(values):
            whole = jnp.sum(value, axis=1, keepdims=True)
            packed = packed + jnp.where(lane == sub + NRHS * k, whole, 0.0)
        return jnp.sum(packed, axis=0, keepdims=True)

    def unpack(total, k):
        return jnp.sum(jnp.where(lane == sub + NRHS * k, total, 0.0), axis=1, keepdims=True)

    put_masked(0, [observed[k] * right[k] for k in range(2)])
    wide = lax.broadcasted_iota(jnp.int32, (1, slots * NRHS), 1)
    row_index = jnp.zeros((1, slots * NRHS), jnp.int32)
    col_index = jnp.zeros((1, slots * NRHS), jnp.int32)
    for t in range(slots):
        here = wide // NRHS == t
        row_index = jnp.where(here, rows_s[t] * NRHS, row_index)
        col_index = jnp.where(here, cols_s[t] * NRHS, col_index)
    live = wide // NRHS < count_s[0]
    row_index = jnp.where(live, row_index + wide % NRHS, -1)
    col_index = jnp.where(live, col_index + wide % NRHS, -1)
    step = 64

    def fill(ref, index):
        for start in range(0, ref.shape[0], step):
            at = lax.broadcasted_iota(jnp.int32, (step, slots * NRHS), 0) + start
            ref[start : start + step] = jnp.where(at == index, 1.0, 0.0).astype(BF16)

    fill(hrow, row_index)
    fill(hcol, col_index)
    diag_copy.wait()
    a_index = lax.broadcasted_iota(jnp.int32, (TILE, TILE), 0)
    b_index = lax.broadcasted_iota(jnp.int32, (TILE, TILE), 1)
    for k in range(2):
        block = diag[k].astype(F32)
        sym[k] = jnp.where(b_index >= a_index, block, block.T).astype(BF16)
    tile_copy.wait()

    def own_terms(masked):
        out = []
        for k in range(2):
            both = jnp.dot(split_rows(masked[k]), sym[k], preferred_element_type=F32)
            out.append(both[:NRHS] + both[NRHS:])
        return out

    masked_b = [observed[k] * right[k] for k in range(2)]
    diag_b = own_terms(masked_b)

    pl.semaphore_wait(barrier, len(peers))

    def gather_upper(it):
        for d in ls:
            col_forward(it, d)
        for d in zs[:-1]:
            row_forward(it, d)

    start_gather(0)
    gather_upper(0)
    col_done(0)
    upper(0)
    for d in zs[-1:]:
        row_forward(0, d)
    row_done(0)
    lower(0)
    quad = jnp.zeros((NRHS, TILE), F32)
    for i in range(2 * nrow):
        quad = quad + rowterm[0, i] * rowbuf[0, i]
    quad = 2.0 * quad
    for k in range(2):
        quad = quad + masked_b[k] * diag_b[k]
    quad = coupling * quad
    for k in range(2):
        quad = quad + noise[k] * right[k] * right[k]
    red_send(0, 0, pack([right[0] * right[0] + right[1] * right[1], quad]))
    for d in reversed(zs):
        row_reduce(0, d)
    for d in [*ls, 0]:
        col_reduce(0, d)
    row_reduce(0, 0)
    red_send(0, 1, red_get(0, 0))
    mirrored = col_final(0)
    red_send(0, 2, red_get(0, 1))
    total = row_final(0) + mirrored
    w = [
        noise[k] * right[k] + observed[k] * (coupling * (total[k] + diag_b[k]))
        for k in range(2)
    ]

    masked_w = [observed[k] * w[k] for k in range(2)]
    put_masked(1, masked_w)
    start_gather(1)
    diag_w = own_terms(masked_w)
    gather_upper(1)
    first = red_get(0, 2)
    rr0, dad0 = unpack(first, 0), unpack(first, 1)
    alpha = rr0 / dad0
    res = [right[k] - alpha * w[k] for k in range(2)]
    red_send(
        1, 0, pack([res[0] * res[0] + res[1] * res[1], res[0] * w[0] + res[1] * w[1]])
    )
    col_done(1)
    upper(1)
    for d in zs[-1:]:
        row_forward(1, d)
    red_send(1, 1, red_get(1, 0))
    row_done(1)
    quad = jnp.zeros((NRHS, TILE), F32)
    for i in range(2 * nrow):
        quad = quad + (rowterm[0, i] - alpha * rowterm[1, i]) * (
            rowbuf[0, i] - alpha * rowbuf[1, i]
        )
    quad = 2.0 * quad
    for k in range(2):
        quad = quad + (masked_b[k] - alpha * masked_w[k]) * (diag_b[k] - alpha * diag_w[k])
    quad = coupling * quad
    for k in range(2):
        quad = quad + noise[k] * res[k] * res[k]
    red_send(2, 0, pack([quad]))
    lower(1)
    red_send(1, 2, red_get(1, 1))
    for d in reversed(zs):
        row_reduce(1, d)
    red_send(2, 1, red_get(2, 0))
    for d in [*ls, 0]:
        col_reduce(1, d)
    row_reduce(1, 0)
    red_send(2, 2, red_get(2, 1))
    mirrored = col_final(1)
    total = row_final(1) + mirrored
    second = red_get(1, 2)
    rr1, rw1 = unpack(second, 0), unpack(second, 1)
    beta = rr1 / rr0
    u = [
        noise[k] * w[k] + observed[k] * (coupling * (total[k] + diag_w[k]))
        for k in range(2)
    ]
    third = unpack(red_get(2, 2), 0)
    dad1 = third + 2.0 * beta * rw1 + beta * beta * dad0
    alpha1 = rr1 / dad1
    for k in range(2):
        here = slice(k * TILE, (k + 1) * TILE)
        direction = res[k] + beta * right[k]
        image = (w[k] - alpha * u[k]) + beta * w[k]
        sol_ref[:, here] = alpha * right[k] + alpha1 * direction
        res_ref[:, here] = res[k] - alpha1 * image
    for copy in pending:
        copy.wait_send()


def local(
    rparts,
    cparts,
    right_sides,
    noise_var,
    observed,
    tile_data,
    diag_tiles,
    tile_rows,
    tile_cols,
    tile_count,
):
    slots = tile_data.shape[2]
    nzh, nx, nc = rparts
    ny, nzl = cparts
    nrow, ncol = nzh * nx * nc, ny * nzl
    vmem = pl.BlockSpec(memory_space=pltpu.VMEM)
    smem = pl.BlockSpec(memory_space=pltpu.SMEM)
    hbm = pl.BlockSpec(memory_space=pl.ANY)
    dma = pltpu.SemaphoreType.DMA
    chunk = (2, NRHS, TILE)
    shape = jax.ShapeDtypeStruct(right_sides.shape, F32)
    return pl.pallas_call(
        functools.partial(kernel, rparts, cparts),
        out_shape=(shape, shape),
        in_specs=[vmem, vmem, vmem, hbm, hbm, smem, smem, smem],
        out_specs=(vmem, vmem),
        scratch_shapes=[
            pltpu.VMEM((slots, TILE, TILE), BF16),
            pltpu.VMEM((2, TILE, TILE), BF16),
            pltpu.VMEM((2, TILE, TILE), BF16),
            pltpu.VMEM((2 * nrow * NRHS, slots * NRHS), BF16),
            pltpu.VMEM((2 * ncol * NRHS, slots * NRHS), BF16),
            pltpu.VMEM((2, 2 * nrow, NRHS, TILE), F32),
            pltpu.VMEM((2, 2 * ncol, NRHS, TILE), F32),
            pltpu.VMEM((2 * nrow, 2 * NRHS, TILE), BF16),
            pltpu.VMEM((2 * ncol, 2 * NRHS, TILE), BF16),
            pltpu.VMEM((slots, 2 * NRHS, TILE), BF16),
            pltpu.VMEM((2, 2 * nrow, NRHS, TILE), F32),
            pltpu.VMEM((2, 2 * ncol, NRHS, TILE), F32),
            pltpu.VMEM((2, nzh, nx * nc, *chunk), F32),
            pltpu.VMEM((2, nzh, *chunk), F32),
            pltpu.VMEM((2, nzh, *chunk), F32),
            pltpu.VMEM((2, nzl, ny, *chunk), F32),
            pltpu.VMEM((2, nzl, *chunk), F32),
            pltpu.VMEM((2, nzl, *chunk), F32),
            pltpu.VMEM((3, 3, 1, TILE), F32),
            pltpu.VMEM((3, 3, max(16, nx * nc), 1, TILE), F32),
            dma((2,)),
            dma((2, 2, nzh)),
            dma((2, 2, nzh, nx * nc)),
            dma((2, 2, nzl)),
            dma((2, 2, nzl, ny)),
            dma((2, 2, nzh, nx * nc)),
            dma((2, 2, nzh)),
            dma((2, 2, nzl, ny)),
            dma((2, 2, nzl)),
            dma((2, 3, 3, 16)),
        ],
        compiler_params=pltpu.CompilerParams(
            collective_id=0, has_side_effects=True, vmem_limit_bytes=48 << 20
        ),
        name="solve",
    )(
        right_sides,
        noise_var.reshape(1, -1),
        observed.reshape(1, -1),
        diag_tiles,
        tile_data.reshape(slots, TILE, TILE),
        tile_rows.reshape(slots),
        tile_cols.reshape(slots),
        tile_count.reshape(1),
    )


def solution(mesh):
    return jax.shard_map(
        functools.partial(local, ROW_PARTS, COL_PARTS),
        mesh=mesh,
        in_specs=(
            P(None, ("row", "col")),
            P(("row", "col")),
            P(("row", "col")),
            P("row", "col", None, None, None),
            P(("row", "col"), None, None),
            P("row", "col", None),
            P("row", "col", None),
            P("row", "col"),
        ),
        out_specs=(P(None, ("row", "col")), P(None, ("row", "col"))),
        check_vma=False,
    )
```

time: 863 us -> 79.2 us (0.09)
  blocking collectives: 492 us -> 0 us
  waiting for transfers between devices: 337 us -> 0 us
  Pallas kernels: 0 us -> 73.7 us
  between operations: 14.6 us -> 1.35 us
  matrix products: 9.38 us -> 0 us
    reduce_scatter x4 -> x0, waiting for transfers between devices: 337 us -> none  [the longest x2 243 us: local(): lax.psum_scatter(row_terms.reshape(rhs_count, row_devices * piece_len), '...]
    psum x3 -> x0, blocking collectives: 304 us -> none  [the longest x2 202 us: residual_norms(): return lax.psum(jnp.sum(residual * residual, axis=1), ('row', 'col'))]
    all_gather x4 -> x0, blocking collectives: 188 us -> none  [the longest x2 118 us: local(): by_row = lax.all_gather(masked, 'row', axis=1, tiled=True)]
    pallas_call x0 -> x1, Pallas kernels: none -> 73.7 us  [local(): pl.pallas_call(functools.partial(kernel, rparts, cparts), out_shape=(shap...]
    dot_general x12 -> x0, matrix products: 9.38 us -> none  [the longest x2 3.53 us: local(): jnp.einsum('tab,stb->sta', local_tiles, jnp.take(by_col, picks_col, axis=...]
  transfers between devices with their start and end apart: 4 -> 0, of which waited for: 4 -> 0; matrix products, arithmetic and copies ran while one was open for 1% -> 0% of each run, Pallas kernels for 0% -> 0%
where the time goes in v1:
time: 79.2 us; the launch traced here: 79 us
  Pallas kernels  73.7 us (93%)
  local copies, waits for them, and re-layouts  3.94 us (5%)
  between operations  1.35 us (2%)
    pallas_call x1, Pallas kernels, local(): pl.pallas_call(functools.partial(kernel, rparts, cparts), out_shape=(shap...  73.7 us
    unnamed x16, local copies, waits for them, and re-layouts  3.94 us

profile of v1, /device:TPU:1, one launch (start us, length us, event | category | flops | bytes accessed | tf_op | source)
XLA Modules:
  0.0 79.0 jit_solution(2989155196432286570)
XLA Ops:
  0.6 0.0 copy-start.2
  1.3 0.0 copy-start.4
  1.3 0.0 copy-start.6
  1.3 0.0 copy-start.3
  1.3 0.0 copy-start.5
  1.3 0.0 copy-done.2
  1.4 0.6 copy-done.4
  2.0 0.0 copy-done.6
  2.0 0.0 copy-done.3
  2.0 0.0 copy-done.5
  2.0 0.0 copy-start
  2.0 1.2 %copy-done = bf16[1,1,32,128,128]{4,3,2,1,0:T(8,128)(2,1)S(1)} copy-done((bf16[1,1,32,128,128]{4,3,2,1,0:T(8,128)(2,1)S(1)}, bf16[1,1,32,128,128]{4,3,2,1,0:T(8,128)(2,1)}, u32[]{:S(2)}) %copy-start) | copy-done | bytes 1048600
  3.2 0.0 copy-start.1
  3.2 0.8 %copy-done.1 = bf16[2,128,128]{2,1,0:T(8,128)(2,1)S(1)} copy-done((bf16[2,128,128]{2,1,0:T(8,128)(2,1)S(1)}, bf16[2,128,128]{2,1,0:T(8,128)(2,1)}, u32[]{:S(2)}) %copy-start.1) | copy-done | bytes 65560
  4.1 73.7 %solve.1 = (f32[8,256]{1,0:T(8,128)S(1)}, f32[8,256]{1,0:T(8,128)S(1)}) custom-call(f32[8,256]{1,0:T(8,128)S(1)} %copy-done.2, f32[1,256]{1,0:T(1,128)S(1)} %bitcast.8, s32[1,256]{1,0:T(1,128)S(1)} %bitcast.9, bf16[2,128,128]{2,1,0:T(8,128)(2,1)S(1)} %copy-done.1, bf16[32,128,128]{2,1,0:T(8,128)(2,1)S(1)} %bitcast.7, s32[32]{0:T(128)S(1)} %bitcast.10, ...), custom_call_target="tpu_custom_call" | custom-call | tf_op jit(solution)/shard_map/solve/pallas_call | solution.py:469
  77.8 0.6 copy.13
  78.4 0.6 copy.14
Async XLA Ops:
  0.6 0.7 copy-start.2
  1.3 0.7 copy-start.4
  1.3 0.7 copy-start.6
  1.3 0.7 copy-start.3
  1.3 0.7 copy-start.5
  2.0 1.2 %copy-start = (bf16[1,1,32,128,128]{4,3,2,1,0:T(8,128)(2,1)S(1)}, bf16[1,1,32,128,128]{4,3,2,1,0:T(8,128)(2,1)}, u32[]{:S(2)}) copy-start(bf16[1,1,32,128,128]{4,3,2,1,0:T(8,128)(2,1)} %param.11) | copy-start | bytes 3145732
  3.2 0.8 %copy-start.1 = (bf16[2,128,128]{2,1,0:T(8,128)(2,1)S(1)}, bf16[2,128,128]{2,1,0:T(8,128)(2,1)}, u32[]{:S(2)}) copy-start(bf16[2,128,128]{2,1,0:T(8,128)(2,1)} %diag_hbm.1) | copy-start | bytes 196612

commit v2 on v1

v2 whole, which is shorter than its diff:
```python
import functools
import math

import jax
import jax.numpy as jnp
from jax import lax
from jax.experimental import pallas as pl
from jax.experimental.pallas import tpu as pltpu
from jax.sharding import PartitionSpec as P

TILE = 128
COUPLED = 32
NRHS = 8
MESH = pl.DeviceIdType.MESH
ROW_PARTS = (4, 4, 2)
COL_PARTS = (4, 4)
F32 = jnp.float32
BF16 = jnp.bfloat16


def split_rows(value):
    high = value.astype(BF16).astype(F32)
    return jnp.concatenate([high, value - high], axis=0).astype(BF16)


def near_first(size):
    return sorted(range(1, size), key=lambda d: min(d, size - d))


def kernel(
    rparts,
    cparts,
    rs_hbm,
    noise_hbm,
    obs_hbm,
    diag_hbm,
    tile_hbm,
    rows_hbm,
    cols_hbm,
    count_hbm,
    sol_ref,
    res_ref,
    rs_ref,
    noise_ref,
    obs_ref,
    rows_s,
    cols_s,
    count_s,
    tiles,
    diag,
    sym,
    hrow,
    hcol,
    rowbuf,
    colbuf,
    rowsplit,
    colsplit,
    gath,
    rowterm,
    colterm,
    xrecv,
    zsend,
    frecv,
    zrecv,
    yrecv,
    lsend,
    lrecv,
    red_src,
    red_dst,
    local_sem,
    sent_sem,
    agz_sem,
    agx_sem,
    agl_sem,
    agy_sem,
    rsx_sem,
    rsf_sem,
    rsz_sem,
    rcy_sem,
    rcl_sem,
    red_sem,
):
    nzh, nx, nc = rparts
    ny, nzl = cparts
    nrow, ncol = nzh * nx * nc, ny * nzl
    slots = tile_hbm.shape[0]
    coupling = 1.0 / (2.0 * math.sqrt(TILE * (2 * COUPLED + 1)))

    row = lax.axis_index("row")
    col = lax.axis_index("col")
    zh, x, core = row // (nx * nc), row // nc % nx, row % nc
    y, zl = col // nzl, col % nzl

    def row_at(dz, dx, dc):
        return (
            lax.rem(zh + dz, nzh) * (nx * nc)
            + lax.rem(x + dx, nx) * nc
            + lax.rem(core + dc, nc)
        )

    def col_at(dy, dl):
        return lax.rem(y + dy, ny) * nzl + lax.rem(zl + dl, nzl)

    def row_from(dz, dx, dc):
        return row_at(nzh - dz, nx - dx, nc - dc)

    def col_from(dy, dl):
        return col_at(ny - dy, nzl - dl)

    plane = [(dx, dc) for dx in range(nx) for dc in range(nc) if dx or dc]
    plane = sorted(plane, key=lambda p: -min(p[0], nx - p[0]))
    line = [(dz, dl) for dz in range(nzh) for dl in range(nzl) if dz or dl]
    line = sorted(line, key=lambda p: -min(p[0] * nzl + p[1], nzh * nzl - p[0] * nzl - p[1]))
    ys, ls = near_first(ny), list(range(1, nzl))
    near = sorted({1, nzh - 1} - {0})
    far = 2 if nzh == 4 else None
    groups = [0, *near] + ([far] if far else [])

    barrier = pltpu.get_barrier_semaphore()
    peers = [(row_at(d, 0, 0), col) for d in near]
    peers += [(row, col_at(0, d)) for d in ls]
    peers += [(row_at(0, dx, dc), col) for dx, dc in plane]
    peers += [(row, col_at(dy, 0)) for dy in ys]
    for peer in peers:
        pl.semaphore_signal(barrier, inc=1, device_id=peer, device_id_type=MESH)

    def remote(src, dst, kind, sem, device):
        return pltpu.make_async_remote_copy(
            src_ref=src,
            dst_ref=dst,
            send_sem=sent_sem.at[kind],
            recv_sem=sem,
            device_id=device,
            device_id_type=MESH,
        )

    def send(src, dst, kind, sem, device):
        remote(src, dst, kind, sem, device).start()

    def arrive(dst, sem):
        remote(dst, dst, 0, sem, (row, col)).wait_recv()

    def sent(src, kind):
        remote(src, src, kind, agz_sem.at[0, 0], (row, col)).wait_send()

    inputs = (
        (rs_hbm, rs_ref),
        (obs_hbm, obs_ref),
        (noise_hbm, noise_ref),
        (rows_hbm, rows_s),
        (cols_hbm, cols_s),
        (count_hbm, count_s),
        (diag_hbm, diag),
        (tile_hbm, tiles),
    )
    inputs = [
        pltpu.make_async_copy(src, dst, local_sem.at[k])
        for k, (src, dst) in enumerate(inputs)
    ]
    for copy in inputs:
        copy.start()
    for copy in inputs[:6]:
        copy.wait()

    observed = [obs_ref[:, k * TILE : (k + 1) * TILE].astype(F32) for k in range(2)]
    noise = [noise_ref[:, k * TILE : (k + 1) * TILE] for k in range(2)]
    right = [rs_ref[:, k * TILE : (k + 1) * TILE] for k in range(2)]

    def chunk_row(it, r):
        return rowbuf.at[it, pl.ds(2 * r, 2)]

    def chunk_col(it, c):
        return colbuf.at[it, pl.ds(2 * c, 2)]

    def put_masked(it, masked):
        for k in range(2):
            rowbuf[it, 2 * row + k] = masked[k]
            colbuf[it, 2 * col + k] = masked[k]

    def start_gather(it):
        mine_r, mine_c = chunk_row(it, row), chunk_col(it, col)
        for n, d in enumerate(near):
            send(mine_r, mine_r, 0, agz_sem.at[it, n], (row_at(d, 0, 0), col))
        for d in ls:
            send(mine_c, mine_c, 1, agl_sem.at[it, d - 1], (row, col_at(0, d)))
        for d in ys:
            send(mine_c, mine_c, 2, agy_sem.at[it], (row, col_at(d, 0)))
        for dx, dc in plane:
            send(mine_r, mine_r, 3, agx_sem.at[it], (row_at(0, dx, dc), col))

    def col_forward(it, d):
        got = chunk_col(it, col_from(0, d))
        arrive(got, agl_sem.at[it, d - 1])
        for dy in ys:
            send(got, got, 2, agy_sem.at[it], (row, col_at(dy, 0)))

    def to_plane(it, got):
        for dx, dc in plane:
            send(got, got, 3, agx_sem.at[it], (row_at(0, dx, dc), col))

    def near_arrive(it):
        for n, d in enumerate(near):
            r = row_from(d, 0, 0)
            arrive(chunk_row(it, r), agz_sem.at[it, n])
            if far:
                half = rowbuf.at[it, 2 * r + n]
                send(half, half, 0, agz_sem.at[it, 2], (row_at(d, 0, 0), col))

    def near_forward(it):
        for d in near:
            to_plane(it, chunk_row(it, row_from(d, 0, 0)))

    def far_forward(it):
        if far:
            got = chunk_row(it, row_from(far, 0, 0))
            arrive(got, agz_sem.at[it, 2])
            to_plane(it, got)

    def col_done(it):
        arrive(colbuf.at[it, : 2 * (ny - 1) * nzl], agy_sem.at[it])

    def row_done(it):
        arrive(rowbuf.at[it, : 2 * len(plane) * nzh], agx_sem.at[it])

    def product(hot, value):
        high = value.astype(BF16)
        low = (value - high.astype(F32)).astype(BF16)
        both = jnp.concatenate([high, low], axis=1)
        sums = jnp.dot(hot, both, preferred_element_type=F32)
        return sums[:, :TILE] + sums[:, TILE:]

    def terms(picks, pieces, contract):
        for t in range(slots):
            gath[t] = pieces[picks[t]]
        out = lax.dot_general(
            gath[...],
            tiles[...],
            (((2,), (contract,)), ((0,), (0,))),
            preferred_element_type=F32,
        )
        return (out[:, :NRHS] + out[:, NRHS:]).reshape(slots * NRHS, TILE)

    def upper(it):
        for j in range(2 * ncol):
            colsplit[j] = split_rows(colbuf[it, j])
        value = terms(cols_s, colsplit, 2)
        rowterm[it] = product(hrow[...], value).reshape(2 * nrow, NRHS, TILE)
        for dz in reversed(groups):
            for p, (dx, dc) in enumerate(plane):
                send(
                    rowterm.at[it, pl.ds(2 * row_at(dz, dx, dc), 2)],
                    xrecv.at[it, dz, p],
                    4,
                    rsx_sem.at[it, dz],
                    (row_at(0, dx, dc), col),
                )

    def lower(it):
        for i in range(2 * nrow):
            rowsplit[i] = split_rows(rowbuf[it, i])
        value = terms(rows_s, rowsplit, 1)
        colterm[it] = product(hcol[...], value).reshape(2 * ncol, NRHS, TILE)
        for dl in [*ls, 0]:
            for dy in ys:
                send(
                    colterm.at[it, pl.ds(2 * col_at(dy, dl), 2)],
                    yrecv.at[it, dl, dy - 1],
                    5,
                    rcy_sem.at[it, dl],
                    (row, col_at(dy, 0)),
                )

    def plane_sum(it, dz):
        arrive(xrecv.at[it, dz], rsx_sem.at[it, dz])
        total = rowterm[it, pl.ds(2 * row_at(dz, 0, 0), 2)]
        for p in range(len(plane)):
            total = total + xrecv[it, dz, p]
        return total

    def far_reduce(it):
        if far:
            zsend[it, far] = plane_sum(it, far)
            for n, d in enumerate(near):
                send(
                    zsend.at[it, far, n],
                    frecv.at[it, n],
                    6,
                    rsf_sem.at[it, n],
                    (row_at(d, 0, 0), col),
                )

    def near_reduce(it):
        sums = [plane_sum(it, d) for d in near]
        for n, d in enumerate(near):
            zsend[it, d] = sums[n]
            if far:
                arrive(frecv.at[it, n], rsf_sem.at[it, n])
                zsend[it, d, n] = sums[n][n] + frecv[it, n]
            send(zsend.at[it, d], zrecv.at[it, n], 6, rsz_sem.at[it], (row_at(d, 0, 0), col))

    def col_reduce(it, dl):
        arrive(yrecv.at[it, dl], rcy_sem.at[it, dl])
        total = colterm[it, pl.ds(2 * col_at(0, dl), 2)]
        for dy in ys:
            total = total + yrecv[it, dl, dy - 1]
        lsend[it, dl] = total
        if dl:
            send(
                lsend.at[it, dl], lrecv.at[it, dl - 1], 7, rcl_sem.at[it], (row, col_at(0, dl))
            )

    def row_final(it):
        total = plane_sum(it, 0)
        arrive(zrecv.at[it], rsz_sem.at[it])
        for n in range(len(near)):
            total = total + zrecv[it, n]
        return total

    def col_final(it):
        total = lsend[it, 0]
        arrive(lrecv.at[it], rcl_sem.at[it])
        for d in ls:
            total = total + lrecv[it, d - 1]
        return total

    lane = lax.broadcasted_iota(jnp.int32, (NRHS, TILE), 1)
    sub = lax.broadcasted_iota(jnp.int32, (NRHS, TILE), 0)
    stages = (
        [(row_at(0, dx, dc), col) for dx, dc in plane],
        [(row, col_at(dy, 0)) for dy in ys],
        [(row_at(dz, 0, 0), col_at(0, dl)) for dz, dl in line],
    )
    first_slot = (0, len(plane), len(plane) + len(ys))

    def red_send(r, stage, value):
        red_src[r, stage] = value
        for n, device in enumerate(stages[stage]):
            send(
                red_src.at[r, stage],
                red_dst.at[r, first_slot[stage] + n],
                8,
                red_sem.at[r, stage],
                device,
            )

    def red_get(r, stage):
        count = len(stages[stage])
        arrive(red_dst.at[r, pl.ds(first_slot[stage], count)], red_sem.at[r, stage])
        total = red_src[r, stage]
        for n in range(count):
            total = total + red_dst[r, first_slot[stage] + n]
        return total

    def pack(values):
        packed = jnp.zeros((NRHS, TILE), F32)
        for k, value in enumerate(values):
            whole = jnp.sum(value, axis=1, keepdims=True)
            packed = packed + jnp.where(lane == sub + NRHS * k, whole, 0.0)
        return jnp.sum(packed, axis=0, keepdims=True)

    def unpack(total, k):
        return jnp.sum(jnp.where(lane == sub + NRHS * k, total, 0.0), axis=1, keepdims=True)

    masked_b = [observed[k] * right[k] for k in range(2)]
    put_masked(0, masked_b)

    def hot_matrices():
        wide = lax.broadcasted_iota(jnp.int32, (1, slots * NRHS), 1)
        row_index = jnp.zeros((1, slots * NRHS), jnp.int32)
        col_index = jnp.zeros((1, slots * NRHS), jnp.int32)
        for t in range(slots):
            here = wide // NRHS == t
            row_index = jnp.where(here, rows_s[t] * NRHS, row_index)
            col_index = jnp.where(here, cols_s[t] * NRHS, col_index)
        live = wide // NRHS < count_s[0, 0]
        row_index = jnp.where(live, row_index + wide % NRHS, -1)
        col_index = jnp.where(live, col_index + wide % NRHS, -1)
        step = 64
        for ref, index in ((hrow, row_index), (hcol, col_index)):
            for start in range(0, ref.shape[0], step):
                at = lax.broadcasted_iota(jnp.int32, (step, slots * NRHS), 0) + start
                ref[start : start + step] = jnp.where(at == index, 1.0, 0.0).astype(BF16)

    def own_terms(masked):
        out = []
        for k in range(2):
            both = jnp.dot(split_rows(masked[k]), sym[k], preferred_element_type=F32)
            out.append(both[:NRHS] + both[NRHS:])
        return out

    hot_matrices()
    inputs[6].wait()
    a_index = lax.broadcasted_iota(jnp.int32, (TILE, TILE), 0)
    b_index = lax.broadcasted_iota(jnp.int32, (TILE, TILE), 1)
    for k in range(2):
        block = diag[k].astype(F32)
        sym[k] = jnp.where(b_index >= a_index, block, block.T).astype(BF16)
    diag_b = own_terms(masked_b)
    inputs[7].wait()

    pl.semaphore_wait(barrier, len(peers))

    def gather_upper(it):
        for d in ls:
            col_forward(it, d)
        near_arrive(it)
        near_forward(it)

    start_gather(0)
    gather_upper(0)
    col_done(0)
    upper(0)
    far_forward(0)
    row_done(0)
    quad = jnp.zeros((NRHS, TILE), F32)
    for i in range(2 * nrow):
        quad = quad + rowterm[0, i] * rowbuf[0, i]
    quad = 2.0 * quad
    for k in range(2):
        quad = quad + masked_b[k] * diag_b[k]
    quad = coupling * quad
    for k in range(2):
        quad = quad + noise[k] * right[k] * right[k]
    red_send(0, 0, pack([right[0] * right[0] + right[1] * right[1], quad]))
    lower(0)
    far_reduce(0)
    near_reduce(0)
    red_send(0, 1, red_get(0, 0))
    for d in [*ls, 0]:
        col_reduce(0, d)
    mirrored = col_final(0)
    red_send(0, 2, red_get(0, 1))
    total = row_final(0) + mirrored
    w = [
        noise[k] * right[k] + observed[k] * (coupling * (total[k] + diag_b[k]))
        for k in range(2)
    ]

    masked_w = [observed[k] * w[k] for k in range(2)]
    put_masked(1, masked_w)
    start_gather(1)
    diag_w = own_terms(masked_w)
    gather_upper(1)
    first = red_get(0, 2)
    rr0, dad0 = unpack(first, 0), unpack(first, 1)
    alpha = rr0 / dad0
    res = [right[k] - alpha * w[k] for k in range(2)]
    red_send(
        1, 0, pack([res[0] * res[0] + res[1] * res[1], res[0] * w[0] + res[1] * w[1]])
    )
    col_done(1)
    upper(1)
    far_forward(1)
    red_send(1, 1, red_get(1, 0))
    row_done(1)
    quad = jnp.zeros((NRHS, TILE), F32)
    for i in range(2 * nrow):
        quad = quad + (rowterm[0, i] - alpha * rowterm[1, i]) * (
            rowbuf[0, i] - alpha * rowbuf[1, i]
        )
    quad = 2.0 * quad
    for k in range(2):
        quad = quad + (masked_b[k] - alpha * masked_w[k]) * (diag_b[k] - alpha * diag_w[k])
    quad = coupling * quad
    for k in range(2):
        quad = quad + noise[k] * res[k] * res[k]
    red_send(2, 0, pack([quad]))
    lower(1)
    red_send(1, 2, red_get(1, 1))
    far_reduce(1)
    red_send(2, 1, red_get(2, 0))
    near_reduce(1)
    for d in [*ls, 0]:
        col_reduce(1, d)
    red_send(2, 2, red_get(2, 1))
    mirrored = col_final(1)
    total = row_final(1) + mirrored
    second = red_get(1, 2)
    rr1, rw1 = unpack(second, 0), unpack(second, 1)
    beta = rr1 / rr0
    u = [
        noise[k] * w[k] + observed[k] * (coupling * (total[k] + diag_w[k]))
        for k in range(2)
    ]
    third = unpack(red_get(2, 2), 0)
    dad1 = third + 2.0 * beta * rw1 + beta * beta * dad0
    alpha1 = rr1 / dad1
    for k in range(2):
        here = slice(k * TILE, (k + 1) * TILE)
        direction = res[k] + beta * right[k]
        image = (w[k] - alpha * u[k]) + beta * w[k]
        sol_ref[:, here] = alpha * right[k] + alpha1 * direction
        res_ref[:, here] = res[k] - alpha1 * image

    hops = len(near) * 2 if not far else 2 * (len(near) + 1)
    sent(rowbuf.at[0, : 2 * hops], 0)
    sent(rowbuf.at[0, : 4 * len(ls)], 1)
    sent(rowbuf.at[:, : 2 * (ny - 1) * nzl], 2)
    sent(rowbuf.at[:, : 2 * len(plane) * nzh], 3)
    sent(rowbuf.at[:, : 2 * len(plane) * nzh], 4)
    sent(rowbuf.at[:, : 2 * (ny - 1) * nzl], 5)
    sent(rowbuf.at[0, : 2 * hops], 6)
    sent(rowbuf.at[0, : 4 * len(ls)], 7)
    sent(red_dst, 8)


def local(
    rparts,
    cparts,
    right_sides,
    noise_var,
    observed,
    tile_data,
    diag_tiles,
    tile_rows,
    tile_cols,
    tile_count,
):
    slots = tile_data.shape[2]
    nzh, nx, nc = rparts
    ny, nzl = cparts
    nrow, ncol = nzh * nx * nc, ny * nzl
    plane, near = nx * nc - 1, min(2, nzh - 1)
    vmem = pl.BlockSpec(memory_space=pltpu.VMEM)
    hbm = pl.BlockSpec(memory_space=pl.ANY)
    dma = pltpu.SemaphoreType.DMA
    chunk = (2, NRHS, TILE)
    shape = jax.ShapeDtypeStruct(right_sides.shape, F32)
    return pl.pallas_call(
        functools.partial(kernel, rparts, cparts),
        out_shape=(shape, shape),
        in_specs=[hbm] * 8,
        out_specs=(vmem, vmem),
        scratch_shapes=[
            pltpu.VMEM(right_sides.shape, F32),
            pltpu.VMEM((1, 2 * TILE), F32),
            pltpu.VMEM((1, 2 * TILE), jnp.int32),
            pltpu.SMEM((slots,), jnp.int32),
            pltpu.SMEM((slots,), jnp.int32),
            pltpu.SMEM((1, 1), jnp.int32),
            pltpu.VMEM((slots, TILE, TILE), BF16),
            pltpu.VMEM((2, TILE, TILE), BF16),
            pltpu.VMEM((2, TILE, TILE), BF16),
            pltpu.VMEM((2 * nrow * NRHS, slots * NRHS), BF16),
            pltpu.VMEM((2 * ncol * NRHS, slots * NRHS), BF16),
            pltpu.VMEM((2, 2 * nrow, NRHS, TILE), F32),
            pltpu.VMEM((2, 2 * ncol, NRHS, TILE), F32),
            pltpu.VMEM((2 * nrow, 2 * NRHS, TILE), BF16),
            pltpu.VMEM((2 * ncol, 2 * NRHS, TILE), BF16),
            pltpu.VMEM((slots, 2 * NRHS, TILE), BF16),
            pltpu.VMEM((2, 2 * nrow, NRHS, TILE), F32),
            pltpu.VMEM((2, 2 * ncol, NRHS, TILE), F32),
            pltpu.VMEM((2, nzh, plane, *chunk), F32),
            pltpu.VMEM((2, nzh, *chunk), F32),
            pltpu.VMEM((2, 2, NRHS, TILE), F32),
            pltpu.VMEM((2, near, *chunk), F32),
            pltpu.VMEM((2, nzl, ny - 1, *chunk), F32),
            pltpu.VMEM((2, nzl, *chunk), F32),
            pltpu.VMEM((2, nzl - 1, *chunk), F32),
            pltpu.VMEM((3, 3, 1, TILE), F32),
            pltpu.VMEM((3, plane + ny - 1 + nzh * nzl - 1, 1, TILE), F32),
            dma((8,)),
            dma((9,)),
            dma((2, 3)),
            dma((2,)),
            dma((2, nzl - 1)),
            dma((2,)),
            dma((2, nzh)),
            dma((2, 2)),
            dma((2,)),
            dma((2, nzl)),
            dma((2,)),
            dma((3, 3)),
        ],
        compiler_params=pltpu.CompilerParams(
            collective_id=0, has_side_effects=True, vmem_limit_bytes=67043328
        ),
        name="solve",
    )(
        right_sides,
        noise_var.reshape(1, -1),
        observed.reshape(1, -1),
        diag_tiles,
        tile_data.reshape(slots, TILE, TILE),
        tile_rows.reshape(slots),
        tile_cols.reshape(slots),
        tile_count,
    )


def solution(mesh):
    return jax.shard_map(
        functools.partial(local, ROW_PARTS, COL_PARTS),
        mesh=mesh,
        in_specs=(
            P(None, ("row", "col")),
            P(("row", "col")),
            P(("row", "col")),
            P("row", "col", None, None, None),
            P(("row", "col"), None, None),
            P("row", "col", None),
            P("row", "col", None),
            P("row", "col"),
        ),
        out_specs=(P(None, ("row", "col")), P(None, ("row", "col"))),
        check_vma=False,
    )
```

time: 79.2 us -> 68.4 us (0.86)
  Pallas kernels: 73.7 us -> 64.9 us
  local copies, waits for them, and re-layouts: 3.94 us -> 1.9 us
    pallas_call x1, Pallas kernels: 73.7 us -> 64.9 us  [local(): pl.pallas_call(functools.partial(kernel, rparts, cparts), out_shape=(shap...]
    unnamed x16 -> x4, local copies, waits for them, and re-layouts: 3.94 us -> 1.9 us
where the time goes in v2:
time: 68.4 us; the launch traced here: 68.1 us
  Pallas kernels  64.9 us (95%)
  local copies, waits for them, and re-layouts  1.9 us (3%)
  between operations  1.3 us (2%)
    pallas_call x1, Pallas kernels, local(): pl.pallas_call(functools.partial(kernel, rparts, cparts), out_shape=(shap...  64.9 us
    unnamed x4, local copies, waits for them, and re-layouts  1.9 us

profile of v2, /device:TPU:1, one launch (start us, length us, event | category | flops | bytes accessed | tf_op | source)
XLA Modules:
  0.0 68.1 jit_solution(13903696593157046140)
XLA Ops:
  1.3 64.9 %solve.1 = (f32[8,256]{1,0:T(8,128)}, f32[8,256]{1,0:T(8,128)}) custom-call(f32[8,256]{1,0:T(8,128)} %rs_hbm.1, f32[1,256]{1,0:T(1,128)} %bitcast.6, s32[1,256]{1,0:T(1,128)} %bitcast.7, bf16[2,128,128]{2,1,0:T(8,128)(2,1)} %diag_hbm.1, bf16[32,128,128]{2,1,0:T(8,128)(2,1)} %bitcast.5, s32[32]{0:T(128)} %bitcast.8, s32[32]{0:T(128)} %bitcast.9, ...), custom_call_target="tpu_custom_call" | custom-call | tf_op jit(solution)/shard_map/solve/pallas_call | solution.py:529
  66.2 0.0 copy-start
  66.2 1.3 %copy.13 = f32[8,256]{1,0:T(8,128)} copy(f32[8,256]{1,0:T(8,128)} %get-tuple-element.4) | data formatting | bytes 16384
  67.5 0.0 copy-done
  67.5 0.6 copy.14
Async XLA Ops:
  66.2 1.3 %copy-start = (f32[8,256]{1,0:T(8,128)S(1)}, f32[8,256]{1,0:T(8,128)}, u32[]{:S(2)}) copy-start(f32[8,256]{1,0:T(8,128)} %get-tuple-element.5) | copy-start | bytes 24580

commit v3 on v2

--- a/solution.py
+++ b/solution.py
@@ -59,8 +59,7 @@
     rowterm,
     colterm,
     xrecv,
-    zsend,
-    frecv,
+    psum,
     zrecv,
     yrecv,
     lsend,
@@ -74,7 +73,6 @@
     agl_sem,
     agy_sem,
     rsx_sem,
-    rsf_sem,
     rsz_sem,
     rcy_sem,
     rcl_sem,
@@ -179,10 +177,12 @@
 
     def start_gather(it):
         mine_r, mine_c = chunk_row(it, row), chunk_col(it, col)
+        for d in reversed(ls):
+            send(mine_c, mine_c, 1, agl_sem.at[it, d - 1], (row, col_at(0, d)))
+        if far and it:
+            send(mine_r, mine_r, 0, agz_sem.at[it, 2], (row_at(far, 0, 0), col))
         for n, d in enumerate(near):
             send(mine_r, mine_r, 0, agz_sem.at[it, n], (row_at(d, 0, 0), col))
-        for d in ls:
-            send(mine_c, mine_c, 1, agl_sem.at[it, d - 1], (row, col_at(0, d)))
         for d in ys:
             send(mine_c, mine_c, 2, agy_sem.at[it], (row, col_at(d, 0)))
         for dx, dc in plane:
@@ -202,7 +202,7 @@
         for n, d in enumerate(near):
             r = row_from(d, 0, 0)
             arrive(chunk_row(it, r), agz_sem.at[it, n])
-            if far:
+            if far and not it:
                 half = rowbuf.at[it, 2 * r + n]
                 send(half, half, 0, agz_sem.at[it, 2], (row_at(d, 0, 0), col))
 
@@ -245,7 +245,9 @@
             colsplit[j] = split_rows(colbuf[it, j])
         value = terms(cols_s, colsplit, 2)
         rowterm[it] = product(hrow[...], value).reshape(2 * nrow, NRHS, TILE)
-        for dz in reversed(groups):
+
+    def to_rows(it, which):
+        for dz in which:
             for p, (dx, dc) in enumerate(plane):
                 send(
                     rowterm.at[it, pl.ds(2 * row_at(dz, dx, dc), 2)],
@@ -275,28 +277,9 @@
         total = rowterm[it, pl.ds(2 * row_at(dz, 0, 0), 2)]
         for p in range(len(plane)):
             total = total + xrecv[it, dz, p]
-        return total
-
-    def far_reduce(it):
-        if far:
-            zsend[it, far] = plane_sum(it, far)
-            for n, d in enumerate(near):
-                send(
-                    zsend.at[it, far, n],
-                    frecv.at[it, n],
-                    6,
-                    rsf_sem.at[it, n],
-                    (row_at(d, 0, 0), col),
-                )
-
-    def near_reduce(it):
-        sums = [plane_sum(it, d) for d in near]
-        for n, d in enumerate(near):
-            zsend[it, d] = sums[n]
-            if far:
-                arrive(frecv.at[it, n], rsf_sem.at[it, n])
-                zsend[it, d, n] = sums[n][n] + frecv[it, n]
-            send(zsend.at[it, d], zrecv.at[it, n], 6, rsz_sem.at[it], (row_at(d, 0, 0), col))
+        psum[it, dz] = total
+        if dz:
+            send(psum.at[it, dz], zrecv.at[it, dz - 1], 6, rsz_sem.at[it], (row_at(dz, 0, 0), col))
 
     def col_reduce(it, dl):
         arrive(yrecv.at[it, dl], rcy_sem.at[it, dl])
@@ -310,10 +293,10 @@
             )
 
     def row_final(it):
-        total = plane_sum(it, 0)
+        total = psum[it, 0]
         arrive(zrecv.at[it], rsz_sem.at[it])
-        for n in range(len(near)):
-            total = total + zrecv[it, n]
+        for d in range(nzh - 1):
+            total = total + zrecv[it, d]
         return total
 
     def col_final(it):
@@ -325,12 +308,12 @@
 
     lane = lax.broadcasted_iota(jnp.int32, (NRHS, TILE), 1)
     sub = lax.broadcasted_iota(jnp.int32, (NRHS, TILE), 0)
+    slab = [(dx, dc, dy) for dx, dc in [*plane, (0, 0)] for dy in [*reversed(ys), 0]]
     stages = (
-        [(row_at(0, dx, dc), col) for dx, dc in plane],
-        [(row, col_at(dy, 0)) for dy in ys],
+        [(row_at(0, dx, dc), col_at(dy, 0)) for dx, dc, dy in slab[:-1]],
         [(row_at(dz, 0, 0), col_at(0, dl)) for dz, dl in line],
     )
-    first_slot = (0, len(plane), len(plane) + len(ys))
+    first_slot = (0, len(slab) - 1)
 
     def red_send(r, stage, value):
         red_src[r, stage] = value
@@ -400,21 +383,26 @@
 
     pl.semaphore_wait(barrier, len(peers))
 
-    def gather_upper(it):
-        for d in ls:
-            col_forward(it, d)
-        near_arrive(it)
-        near_forward(it)
+    outer = [far] if far else []
 
     start_gather(0)
-    gather_upper(0)
+    for d in ls:
+        col_forward(0, d)
+    near_arrive(0)
+    near_forward(0)
     col_done(0)
     upper(0)
+    to_rows(0, outer)
     far_forward(0)
+    to_rows(0, [*near, 0])
+    for d in [*outer, *near, 0]:
+        plane_sum(0, d)
     row_done(0)
+    lower(0)
     quad = jnp.zeros((NRHS, TILE), F32)
-    for i in range(2 * nrow):
-        quad = quad + rowterm[0, i] * rowbuf[0, i]
+    for d in groups:
+        for k in range(2):
+            quad = quad + psum[0, d, k] * rowbuf[0, 2 * row_at(d, 0, 0) + k]
     quad = 2.0 * quad
     for k in range(2):
         quad = quad + masked_b[k] * diag_b[k]
@@ -422,15 +410,10 @@
     for k in range(2):
         quad = quad + noise[k] * right[k] * right[k]
     red_send(0, 0, pack([right[0] * right[0] + right[1] * right[1], quad]))
-    lower(0)
-    far_reduce(0)
-    near_reduce(0)
-    red_send(0, 1, red_get(0, 0))
     for d in [*ls, 0]:
         col_reduce(0, d)
-    mirrored = col_final(0)
-    red_send(0, 2, red_get(0, 1))
-    total = row_final(0) + mirrored
+    red_send(0, 1, red_get(0, 0))
+    total = row_final(0) + col_final(0)
     w = [
         noise[k] * right[k] + observed[k] * (coupling * (total[k] + diag_b[k]))
         for k in range(2)
@@ -440,24 +423,30 @@
     put_masked(1, masked_w)
     start_gather(1)
     diag_w = own_terms(masked_w)
-    gather_upper(1)
-    first = red_get(0, 2)
+    for d in ls:
+        col_forward(1, d)
+    near_arrive(1)
+    near_forward(1)
+    col_done(1)
+    upper(1)
+    to_rows(1, [*outer, *near, 0])
+    first = red_get(0, 1)
     rr0, dad0 = unpack(first, 0), unpack(first, 1)
     alpha = rr0 / dad0
     res = [right[k] - alpha * w[k] for k in range(2)]
     red_send(
         1, 0, pack([res[0] * res[0] + res[1] * res[1], res[0] * w[0] + res[1] * w[1]])
     )
-    col_done(1)
-    upper(1)
     far_forward(1)
-    red_send(1, 1, red_get(1, 0))
-    row_done(1)
+    for d in [*outer, *near, 0]:
+        plane_sum(1, d)
     quad = jnp.zeros((NRHS, TILE), F32)
-    for i in range(2 * nrow):
-        quad = quad + (rowterm[0, i] - alpha * rowterm[1, i]) * (
-            rowbuf[0, i] - alpha * rowbuf[1, i]
-        )
+    for d in groups:
+        for k in range(2):
+            block = 2 * row_at(d, 0, 0) + k
+            quad = quad + (psum[0, d, k] - alpha * psum[1, d, k]) * (
+                rowbuf[0, block] - alpha * rowbuf[1, block]
+            )
     quad = 2.0 * quad
     for k in range(2):
         quad = quad + (masked_b[k] - alpha * masked_w[k]) * (diag_b[k] - alpha * diag_w[k])
@@ -465,24 +454,21 @@
     for k in range(2):
         quad = quad + noise[k] * res[k] * res[k]
     red_send(2, 0, pack([quad]))
+    red_send(1, 1, red_get(1, 0))
+    row_done(1)
     lower(1)
-    red_send(1, 2, red_get(1, 1))
-    far_reduce(1)
     red_send(2, 1, red_get(2, 0))
-    near_reduce(1)
     for d in [*ls, 0]:
         col_reduce(1, d)
-    red_send(2, 2, red_get(2, 1))
-    mirrored = col_final(1)
-    total = row_final(1) + mirrored
-    second = red_get(1, 2)
+    total = row_final(1) + col_final(1)
+    second = red_get(1, 1)
     rr1, rw1 = unpack(second, 0), unpack(second, 1)
     beta = rr1 / rr0
     u = [
         noise[k] * w[k] + observed[k] * (coupling * (total[k] + diag_w[k]))
         for k in range(2)
     ]
-    third = unpack(red_get(2, 2), 0)
+    third = unpack(red_get(2, 1), 0)
     dad1 = third + 2.0 * beta * rw1 + beta * beta * dad0
     alpha1 = rr1 / dad1
     for k in range(2):
@@ -492,7 +478,7 @@
         sol_ref[:, here] = alpha * right[k] + alpha1 * direction
         res_ref[:, here] = res[k] - alpha1 * image
 
-    hops = len(near) * 2 if not far else 2 * (len(near) + 1)
+    hops = 2 * (nzh - 1)
     sent(rowbuf.at[0, : 2 * hops], 0)
     sent(rowbuf.at[0, : 4 * len(ls)], 1)
     sent(rowbuf.at[:, : 2 * (ny - 1) * nzl], 2)
@@ -520,9 +506,9 @@
     nzh, nx, nc = rparts
     ny, nzl = cparts
     nrow, ncol = nzh * nx * nc, ny * nzl
-    plane, near = nx * nc - 1, min(2, nzh - 1)
+    plane = nx * nc - 1
     vmem = pl.BlockSpec(memory_space=pltpu.VMEM)
-    hbm = pl.BlockSpec(memory_space=pl.ANY)
+    hbm = pl.BlockSpec(memory_space=pltpu.HBM)
     dma = pltpu.SemaphoreType.DMA
     chunk = (2, NRHS, TILE)
     shape = jax.ShapeDtypeStruct(right_sides.shape, F32)
@@ -552,13 +538,12 @@
             pltpu.VMEM((2, 2 * ncol, NRHS, TILE), F32),
             pltpu.VMEM((2, nzh, plane, *chunk), F32),
             pltpu.VMEM((2, nzh, *chunk), F32),
-            pltpu.VMEM((2, 2, NRHS, TILE), F32),
-            pltpu.VMEM((2, near, *chunk), F32),
+            pltpu.VMEM((2, nzh - 1, *chunk), F32),
             pltpu.VMEM((2, nzl, ny - 1, *chunk), F32),
             pltpu.VMEM((2, nzl, *chunk), F32),
             pltpu.VMEM((2, nzl - 1, *chunk), F32),
-            pltpu.VMEM((3, 3, 1, TILE), F32),
-            pltpu.VMEM((3, plane + ny - 1 + nzh * nzl - 1, 1, TILE), F32),
+            pltpu.VMEM((3, 2, 1, TILE), F32),
+            pltpu.VMEM((3, (plane + 1) * ny - 1 + nzh * nzl - 1, 1, TILE), F32),
             dma((8,)),
             dma((9,)),
             dma((2, 3)),
@@ -566,11 +551,10 @@
             dma((2, nzl - 1)),
             dma((2,)),
             dma((2, nzh)),
-            dma((2, 2)),
             dma((2,)),
             dma((2, nzl)),
             dma((2,)),
-            dma((3, 3)),
+            dma((3, 2)),
         ],
         compiler_params=pltpu.CompilerParams(
             collective_id=0, has_side_effects=True, vmem_limit_bytes=67043328

time: 68.4 us -> 65.8 us (0.962)
  Pallas kernels: 64.9 us -> 62.4 us
    pallas_call x1, Pallas kernels: 64.9 us -> 62.4 us  [local(): pl.pallas_call(functools.partial(kernel, rparts, cparts), out_shape=(shap...]
where the time goes in v3:
time: 65.8 us; the launch traced here: 65.6 us
  Pallas kernels  62.4 us (95%)
  local copies, waits for them, and re-layouts  1.9 us (3%)
  between operations  1.3 us (2%)
    pallas_call x1, Pallas kernels, local(): pl.pallas_call(functools.partial(kernel, rparts, cparts), out_shape=(shap...  62.4 us
    unnamed x4, local copies, waits for them, and re-layouts  1.9 us

profile of v3, /device:TPU:1, one launch (start us, length us, event | category | flops | bytes accessed | tf_op | source)
XLA Modules:
  0.0 65.6 jit_solution(9609720429268611495)
XLA Ops:
  1.3 62.4 %solve.1 = (f32[8,256]{1,0:T(8,128)}, f32[8,256]{1,0:T(8,128)}) custom-call(f32[8,256]{1,0:T(8,128)} %rs_hbm.1, f32[1,256]{1,0:T(1,128)} %bitcast.6, s32[1,256]{1,0:T(1,128)} %bitcast.7, bf16[2,128,128]{2,1,0:T(8,128)(2,1)} %diag_hbm.1, bf16[32,128,128]{2,1,0:T(8,128)(2,1)} %bitcast.5, s32[32]{0:T(128)} %bitcast.8, s32[32]{0:T(128)} %bitcast.9, ...), custom_call_target="tpu_custom_call" | custom-call | tf_op jit(solution)/shard_map/solve/pallas_call | solution.py:515
  63.7 0.0 copy-start
  63.7 1.3 %copy.13 = f32[8,256]{1,0:T(8,128)} copy(f32[8,256]{1,0:T(8,128)} %get-tuple-element.4) | data formatting | bytes 16384
  65.0 0.0 copy-done
  65.0 0.6 copy.14
Async XLA Ops:
  63.7 1.3 %copy-start = (f32[8,256]{1,0:T(8,128)S(1)}, f32[8,256]{1,0:T(8,128)}, u32[]{:S(2)}) copy-start(f32[8,256]{1,0:T(8,128)} %get-tuple-element.5) | copy-start | bytes 24580

commit v4 on v3

--- a/solution.py
+++ b/solution.py
@@ -55,15 +55,13 @@
     colbuf,
     rowsplit,
     colsplit,
-    gath,
+    both,
     rowterm,
     colterm,
     xrecv,
     psum,
     zrecv,
     yrecv,
-    lsend,
-    lrecv,
     red_src,
     red_dst,
     local_sem,
@@ -75,7 +73,6 @@
     rsx_sem,
     rsz_sem,
     rcy_sem,
-    rcl_sem,
     red_sem,
 ):
     nzh, nx, nc = rparts
@@ -110,9 +107,12 @@
     line = [(dz, dl) for dz in range(nzh) for dl in range(nzl) if dz or dl]
     line = sorted(line, key=lambda p: -min(p[0] * nzl + p[1], nzh * nzl - p[0] * nzl - p[1]))
     ys, ls = near_first(ny), list(range(1, nzl))
+    ring = [(dy, dl) for dy in range(ny) for dl in range(nzl) if dy or dl]
+    ring = sorted(ring, key=lambda p: -min(p[0], ny - p[0]) - (2 if p[1] else 0))
     near = sorted({1, nzh - 1} - {0})
     far = 2 if nzh == 4 else None
-    groups = [0, *near] + ([far] if far else [])
+    inner = [*near, 0]
+    outer = [far] if far else []
 
     barrier = pltpu.get_barrier_semaphore()
     peers = [(row_at(d, 0, 0), col) for d in near]
@@ -177,26 +177,30 @@
 
     def start_gather(it):
         mine_r, mine_c = chunk_row(it, row), chunk_col(it, col)
-        for d in reversed(ls):
-            send(mine_c, mine_c, 1, agl_sem.at[it, d - 1], (row, col_at(0, d)))
-        if far and it:
-            send(mine_r, mine_r, 0, agz_sem.at[it, 2], (row_at(far, 0, 0), col))
+        if it:
+            for dy, dl in ring:
+                send(mine_c, mine_c, 2, agy_sem.at[it], (row, col_at(dy, dl)))
+            if far:
+                send(mine_r, mine_r, 0, agz_sem.at[it, 2], (row_at(far, 0, 0), col))
         for n, d in enumerate(near):
             send(mine_r, mine_r, 0, agz_sem.at[it, n], (row_at(d, 0, 0), col))
-        for d in ys:
-            send(mine_c, mine_c, 2, agy_sem.at[it], (row, col_at(d, 0)))
+        if not it:
+            for d in reversed(ls):
+                send(mine_c, mine_c, 1, agl_sem.at[d - 1], (row, col_at(0, d)))
+            for d in ys:
+                send(mine_c, mine_c, 2, agy_sem.at[it], (row, col_at(d, 0)))
         for dx, dc in plane:
-            send(mine_r, mine_r, 3, agx_sem.at[it], (row_at(0, dx, dc), col))
-
-    def col_forward(it, d):
-        got = chunk_col(it, col_from(0, d))
-        arrive(got, agl_sem.at[it, d - 1])
+            send(mine_r, mine_r, 3, agx_sem.at[it, 0], (row_at(0, dx, dc), col))
+
+    def col_forward(d):
+        got = chunk_col(0, col_from(0, d))
+        arrive(got, agl_sem.at[d - 1])
         for dy in ys:
-            send(got, got, 2, agy_sem.at[it], (row, col_at(dy, 0)))
-
-    def to_plane(it, got):
+            send(got, got, 2, agy_sem.at[0], (row, col_at(dy, 0)))
+
+    def to_plane(it, got, late):
         for dx, dc in plane:
-            send(got, got, 3, agx_sem.at[it], (row_at(0, dx, dc), col))
+            send(got, got, 3, agx_sem.at[it, late], (row_at(0, dx, dc), col))
 
     def near_arrive(it):
         for n, d in enumerate(near):
@@ -208,89 +212,100 @@
 
     def near_forward(it):
         for d in near:
-            to_plane(it, chunk_row(it, row_from(d, 0, 0)))
+            to_plane(it, chunk_row(it, row_from(d, 0, 0)), 0)
 
     def far_forward(it):
         if far:
             got = chunk_row(it, row_from(far, 0, 0))
             arrive(got, agz_sem.at[it, 2])
-            to_plane(it, got)
+            to_plane(it, got, 1)
 
     def col_done(it):
-        arrive(colbuf.at[it, : 2 * (ny - 1) * nzl], agy_sem.at[it])
+        count = ncol - 1 if it else (ny - 1) * nzl
+        arrive(colbuf.at[it, : 2 * count], agy_sem.at[it])
+
+    def near_done(it):
+        arrive(rowbuf.at[it, : 2 * len(plane) * len(inner)], agx_sem.at[it, 0])
 
     def row_done(it):
-        arrive(rowbuf.at[it, : 2 * len(plane) * nzh], agx_sem.at[it])
-
-    def product(hot, value):
-        high = value.astype(BF16)
-        low = (value - high.astype(F32)).astype(BF16)
-        both = jnp.concatenate([high, low], axis=1)
-        sums = jnp.dot(hot, both, preferred_element_type=F32)
-        return sums[:, :TILE] + sums[:, TILE:]
+        if far:
+            arrive(rowbuf.at[it, : 2 * len(plane)], agx_sem.at[it, 1])
+
+    def product(hot):
+        sums = jnp.dot(hot, both[...], preferred_element_type=F32)
+        return (sums[:, :TILE] + sums[:, TILE:]).reshape(hot.shape[0] // NRHS, NRHS, TILE)
 
     def terms(picks, pieces, contract):
-        for t in range(slots):
-            gath[t] = pieces[picks[t]]
-        out = lax.dot_general(
-            gath[...],
-            tiles[...],
-            (((2,), (contract,)), ((0,), (0,))),
-            preferred_element_type=F32,
-        )
-        return (out[:, :NRHS] + out[:, NRHS:]).reshape(slots * NRHS, TILE)
+        for t in range(0, slots, 2):
+            left = jnp.concatenate([pieces[picks[t]], pieces[picks[t + 1]]], axis=0)
+            if contract:
+                pair = tiles[t : t + 2].reshape(2 * TILE, TILE)
+            else:
+                pair = jnp.concatenate([tiles[t], tiles[t + 1]], axis=1)
+            sums = lax.dot_general(
+                left, pair, (((1,), (contract,)), ((), ())), preferred_element_type=F32
+            )
+            value = []
+            for k in range(2):
+                part = sums[2 * NRHS * k : 2 * NRHS * (k + 1), TILE * k : TILE * (k + 1)]
+                value.append(part[:NRHS] + part[NRHS:])
+            value = jnp.concatenate(value, axis=0)
+            high = value.astype(BF16)
+            low = (value - high.astype(F32)).astype(BF16)
+            both[t * NRHS : (t + 2) * NRHS] = jnp.concatenate([high, low], axis=1)
 
     def upper(it):
         for j in range(2 * ncol):
             colsplit[j] = split_rows(colbuf[it, j])
-        value = terms(cols_s, colsplit, 2)
-        rowterm[it] = product(hrow[...], value).reshape(2 * nrow, NRHS, TILE)
+        terms(cols_s, colsplit, 1)
+
+    def row_block(dx, dc):
+        return 2 * (lax.rem(x + dx, nx) * nc + lax.rem(core + dc, nc))
 
     def to_rows(it, which):
+        count = 2 * nx * nc * NRHS
+        for dz in which:
+            rowterm[it, dz] = product(hrow[dz * count : (dz + 1) * count])
         for dz in which:
             for p, (dx, dc) in enumerate(plane):
                 send(
-                    rowterm.at[it, pl.ds(2 * row_at(dz, dx, dc), 2)],
+                    rowterm.at[it, dz, pl.ds(row_block(dx, dc), 2)],
                     xrecv.at[it, dz, p],
                     4,
                     rsx_sem.at[it, dz],
                     (row_at(0, dx, dc), col),
                 )
 
+    def split_chunk(it, r):
+        for k in range(2):
+            rowsplit[2 * r + k] = split_rows(rowbuf[it, 2 * r + k])
+
+    def split_plane(it, which):
+        for d in which:
+            for dx in range(nx):
+                for dc in range(nc):
+                    split_chunk(it, row_at(d, dx, dc))
+
     def lower(it):
-        for i in range(2 * nrow):
-            rowsplit[i] = split_rows(rowbuf[it, i])
-        value = terms(rows_s, rowsplit, 1)
-        colterm[it] = product(hcol[...], value).reshape(2 * ncol, NRHS, TILE)
-        for dl in [*ls, 0]:
-            for dy in ys:
-                send(
-                    colterm.at[it, pl.ds(2 * col_at(dy, dl), 2)],
-                    yrecv.at[it, dl, dy - 1],
-                    5,
-                    rcy_sem.at[it, dl],
-                    (row, col_at(dy, 0)),
-                )
+        terms(rows_s, rowsplit, 0)
+        colterm[it] = product(hcol[...])
+        for n, (dy, dl) in enumerate(ring):
+            send(
+                colterm.at[it, pl.ds(2 * col_at(dy, dl), 2)],
+                yrecv.at[it, n],
+                5,
+                rcy_sem.at[it],
+                (row, col_at(dy, dl)),
+            )
 
     def plane_sum(it, dz):
         arrive(xrecv.at[it, dz], rsx_sem.at[it, dz])
-        total = rowterm[it, pl.ds(2 * row_at(dz, 0, 0), 2)]
+        total = rowterm[it, dz, pl.ds(row_block(0, 0), 2)]
         for p in range(len(plane)):
             total = total + xrecv[it, dz, p]
         psum[it, dz] = total
         if dz:
             send(psum.at[it, dz], zrecv.at[it, dz - 1], 6, rsz_sem.at[it], (row_at(dz, 0, 0), col))
-
-    def col_reduce(it, dl):
-        arrive(yrecv.at[it, dl], rcy_sem.at[it, dl])
-        total = colterm[it, pl.ds(2 * col_at(0, dl), 2)]
-        for dy in ys:
-            total = total + yrecv[it, dl, dy - 1]
-        lsend[it, dl] = total
-        if dl:
-            send(
-                lsend.at[it, dl], lrecv.at[it, dl - 1], 7, rcl_sem.at[it], (row, col_at(0, dl))
-            )
 
     def row_final(it):
         total = psum[it, 0]
@@ -300,10 +315,10 @@
         return total
 
     def col_final(it):
-        total = lsend[it, 0]
-        arrive(lrecv.at[it], rcl_sem.at[it])
-        for d in ls:
-            total = total + lrecv[it, d - 1]
+        arrive(yrecv.at[it], rcy_sem.at[it])
+        total = colterm[it, pl.ds(2 * col, 2)]
+        for n in range(ncol - 1):
+            total = total + yrecv[it, n]
         return total
 
     lane = lax.broadcasted_iota(jnp.int32, (NRHS, TILE), 1)
@@ -321,7 +336,7 @@
             send(
                 red_src.at[r, stage],
                 red_dst.at[r, first_slot[stage] + n],
-                8,
+                7,
                 red_sem.at[r, stage],
                 device,
             )
@@ -355,6 +370,8 @@
             here = wide // NRHS == t
             row_index = jnp.where(here, rows_s[t] * NRHS, row_index)
             col_index = jnp.where(here, cols_s[t] * NRHS, col_index)
+        here = 2 * nx * nc * NRHS
+        row_index = (row_index // here + (nzh - zh)) % nzh * here + row_index % here
         live = wide // NRHS < count_s[0, 0]
         row_index = jnp.where(live, row_index + wide % NRHS, -1)
         col_index = jnp.where(live, col_index + wide % NRHS, -1)
@@ -383,26 +400,37 @@
 
     pl.semaphore_wait(barrier, len(peers))
 
-    outer = [far] if far else []
+    def far_pairs():
+        return [((d, k), 2 * row_at(d, 0, 0) + k) for d in outer for k in range(2)]
+
+    def inner_pairs():
+        return [
+            ((d, row_block(dx, dc) + k), 2 * row_at(d, dx, dc) + k)
+            for d in inner
+            for dx in range(nx)
+            for dc in range(nc)
+            for k in range(2)
+        ]
 
     start_gather(0)
     for d in ls:
-        col_forward(0, d)
+        col_forward(d)
     near_arrive(0)
     near_forward(0)
     col_done(0)
     upper(0)
     to_rows(0, outer)
     far_forward(0)
-    to_rows(0, [*near, 0])
-    for d in [*outer, *near, 0]:
+    to_rows(0, inner)
+    near_done(0)
+    split_plane(0, inner)
+    quad = jnp.zeros((NRHS, TILE), F32)
+    for at, block in inner_pairs():
+        quad = quad + rowterm[(0, *at)] * rowbuf[0, block]
+    for d in outer:
         plane_sum(0, d)
-    row_done(0)
-    lower(0)
-    quad = jnp.zeros((NRHS, TILE), F32)
-    for d in groups:
-        for k in range(2):
-            quad = quad + psum[0, d, k] * rowbuf[0, 2 * row_at(d, 0, 0) + k]
+    for at, block in far_pairs():
+        quad = quad + psum[(0, *at)] * rowbuf[0, block]
     quad = 2.0 * quad
     for k in range(2):
         quad = quad + masked_b[k] * diag_b[k]
@@ -410,8 +438,11 @@
     for k in range(2):
         quad = quad + noise[k] * right[k] * right[k]
     red_send(0, 0, pack([right[0] * right[0] + right[1] * right[1], quad]))
-    for d in [*ls, 0]:
-        col_reduce(0, d)
+    for d in inner:
+        plane_sum(0, d)
+    row_done(0)
+    split_plane(0, outer)
+    lower(0)
     red_send(0, 1, red_get(0, 0))
     total = row_final(0) + col_final(0)
     w = [
@@ -423,13 +454,15 @@
     put_masked(1, masked_w)
     start_gather(1)
     diag_w = own_terms(masked_w)
-    for d in ls:
-        col_forward(1, d)
     near_arrive(1)
     near_forward(1)
     col_done(1)
     upper(1)
-    to_rows(1, [*outer, *near, 0])
+    to_rows(1, outer)
+    far_forward(1)
+    to_rows(1, inner)
+    near_done(1)
+    split_plane(1, inner)
     first = red_get(0, 1)
     rr0, dad0 = unpack(first, 0), unpack(first, 1)
     alpha = rr0 / dad0
@@ -437,16 +470,17 @@
     red_send(
         1, 0, pack([res[0] * res[0] + res[1] * res[1], res[0] * w[0] + res[1] * w[1]])
     )
-    far_forward(1)
-    for d in [*outer, *near, 0]:
+    quad = jnp.zeros((NRHS, TILE), F32)
+    for at, block in inner_pairs():
+        quad = quad + (rowterm[(0, *at)] - alpha * rowterm[(1, *at)]) * (
+            rowbuf[0, block] - alpha * rowbuf[1, block]
+        )
+    for d in outer:
         plane_sum(1, d)
-    quad = jnp.zeros((NRHS, TILE), F32)
-    for d in groups:
-        for k in range(2):
-            block = 2 * row_at(d, 0, 0) + k
-            quad = quad + (psum[0, d, k] - alpha * psum[1, d, k]) * (
-                rowbuf[0, block] - alpha * rowbuf[1, block]
-            )
+    for at, block in far_pairs():
+        quad = quad + (psum[(0, *at)] - alpha * psum[(1, *at)]) * (
+            rowbuf[0, block] - alpha * rowbuf[1, block]
+        )
     quad = 2.0 * quad
     for k in range(2):
         quad = quad + (masked_b[k] - alpha * masked_w[k]) * (diag_b[k] - alpha * diag_w[k])
@@ -455,11 +489,12 @@
         quad = quad + noise[k] * res[k] * res[k]
     red_send(2, 0, pack([quad]))
     red_send(1, 1, red_get(1, 0))
+    for d in inner:
+        plane_sum(1, d)
     row_done(1)
+    split_plane(1, outer)
     lower(1)
     red_send(2, 1, red_get(2, 0))
-    for d in [*ls, 0]:
-        col_reduce(1, d)
     total = row_final(1) + col_final(1)
     second = red_get(1, 1)
     rr1, rw1 = unpack(second, 0), unpack(second, 1)
@@ -480,14 +515,13 @@
 
     hops = 2 * (nzh - 1)
     sent(rowbuf.at[0, : 2 * hops], 0)
-    sent(rowbuf.at[0, : 4 * len(ls)], 1)
-    sent(rowbuf.at[:, : 2 * (ny - 1) * nzl], 2)
+    sent(rowbuf.at[0, : 2 * len(ls)], 1)
+    sent(rowbuf.at[0, : 2 * ((ny - 1) * nzl + ncol - 1)], 2)
     sent(rowbuf.at[:, : 2 * len(plane) * nzh], 3)
     sent(rowbuf.at[:, : 2 * len(plane) * nzh], 4)
-    sent(rowbuf.at[:, : 2 * (ny - 1) * nzl], 5)
+    sent(rowbuf.at[0, : 4 * (ncol - 1)], 5)
     sent(rowbuf.at[0, : 2 * hops], 6)
-    sent(rowbuf.at[0, : 4 * len(ls)], 7)
-    sent(red_dst, 8)
+    sent(red_dst, 7)
 
 
 def local(
@@ -533,26 +567,23 @@
             pltpu.VMEM((2, 2 * ncol, NRHS, TILE), F32),
             pltpu.VMEM((2 * nrow, 2 * NRHS, TILE), BF16),
             pltpu.VMEM((2 * ncol, 2 * NRHS, TILE), BF16),
-            pltpu.VMEM((slots, 2 * NRHS, TILE), BF16),
-            pltpu.VMEM((2, 2 * nrow, NRHS, TILE), F32),
+            pltpu.VMEM((slots * NRHS, 2 * TILE), BF16),
+            pltpu.VMEM((2, nzh, 2 * nx * nc, NRHS, TILE), F32),
             pltpu.VMEM((2, 2 * ncol, NRHS, TILE), F32),
             pltpu.VMEM((2, nzh, plane, *chunk), F32),
             pltpu.VMEM((2, nzh, *chunk), F32),
             pltpu.VMEM((2, nzh - 1, *chunk), F32),
-            pltpu.VMEM((2, nzl, ny - 1, *chunk), F32),
-            pltpu.VMEM((2, nzl, *chunk), F32),
-            pltpu.VMEM((2, nzl - 1, *chunk), F32),
+            pltpu.VMEM((2, ncol - 1, *chunk), F32),
             pltpu.VMEM((3, 2, 1, TILE), F32),
             pltpu.VMEM((3, (plane + 1) * ny - 1 + nzh * nzl - 1, 1, TILE), F32),
             dma((8,)),
-            dma((9,)),
+            dma((8,)),
             dma((2, 3)),
-            dma((2,)),
-            dma((2, nzl - 1)),
+            dma((2, 2)),
+            dma((nzl - 1,)),
             dma((2,)),
             dma((2, nzh)),
             dma((2,)),
-            dma((2, nzl)),
             dma((2,)),
             dma((3, 2)),
         ],

time: 65.8 us -> 65.8 us (level)
  no operation moved by 1% of the time
where the time goes in v4:
time: 65.8 us; the launch traced here: 65.6 us
  Pallas kernels  62.4 us (95%)
  local copies, waits for them, and re-layouts  1.9 us (3%)
  between operations  1.3 us (2%)
    pallas_call x1, Pallas kernels, local(): pl.pallas_call(functools.partial(kernel, rparts, cparts), out_shape=(shap...  62.4 us
    unnamed x4, local copies, waits for them, and re-layouts  1.9 us

profile of v4, /device:TPU:1, one launch (start us, length us, event | category | flops | bytes accessed | tf_op | source)
XLA Modules:
  0.0 65.6 jit_solution(12847999692232640953)
XLA Ops:
  1.3 62.4 %solve.1 = (f32[8,256]{1,0:T(8,128)}, f32[8,256]{1,0:T(8,128)}) custom-call(f32[8,256]{1,0:T(8,128)} %rs_hbm.1, f32[1,256]{1,0:T(1,128)} %bitcast.6, s32[1,256]{1,0:T(1,128)} %bitcast.7, bf16[2,128,128]{2,1,0:T(8,128)(2,1)} %diag_hbm.1, bf16[32,128,128]{2,1,0:T(8,128)(2,1)} %bitcast.5, s32[32]{0:T(128)} %bitcast.8, s32[32]{0:T(128)} %bitcast.9, ...), custom_call_target="tpu_custom_call" | custom-call | tf_op jit(solution)/shard_map/solve/pallas_call | solution.py:549
  63.7 0.0 copy-start
  63.7 1.3 %copy.13 = f32[8,256]{1,0:T(8,128)} copy(f32[8,256]{1,0:T(8,128)} %get-tuple-element.4) | data formatting | bytes 16384
  65.0 0.0 copy-done
  65.0 0.6 copy.14
Async XLA Ops:
  63.7 1.3 %copy-start = (f32[8,256]{1,0:T(8,128)S(1)}, f32[8,256]{1,0:T(8,128)}, u32[]{:S(2)}) copy-start(f32[8,256]{1,0:T(8,128)} %get-tuple-element.5) | copy-start | bytes 24580

commit v5 on v4

--- a/solution.py
+++ b/solution.py
@@ -12,6 +12,7 @@
 COUPLED = 32
 NRHS = 8
 MESH = pl.DeviceIdType.MESH
+DIRECT = (True, False)
 ROW_PARTS = (4, 4, 2)
 COL_PARTS = (4, 4)
 F32 = jnp.float32
@@ -38,8 +39,7 @@
     rows_hbm,
     cols_hbm,
     count_hbm,
-    sol_ref,
-    res_ref,
+    out_ref,
     rs_ref,
     noise_ref,
     obs_ref,
@@ -62,6 +62,8 @@
     psum,
     zrecv,
     yrecv,
+    lsend,
+    lrecv,
     red_src,
     red_dst,
     local_sem,
@@ -73,6 +75,7 @@
     rsx_sem,
     rsz_sem,
     rcy_sem,
+    rcl_sem,
     red_sem,
 ):
     nzh, nx, nc = rparts
@@ -177,26 +180,22 @@
 
     def start_gather(it):
         mine_r, mine_c = chunk_row(it, row), chunk_col(it, col)
-        if it:
-            for dy, dl in ring:
-                send(mine_c, mine_c, 2, agy_sem.at[it], (row, col_at(dy, dl)))
-            if far:
-                send(mine_r, mine_r, 0, agz_sem.at[it, 2], (row_at(far, 0, 0), col))
+        for d in reversed(ls):
+            send(mine_c, mine_c, 1, agl_sem.at[it, d - 1], (row, col_at(0, d)))
+        if it and far:
+            send(mine_r, mine_r, 0, agz_sem.at[it, 2], (row_at(far, 0, 0), col))
         for n, d in enumerate(near):
             send(mine_r, mine_r, 0, agz_sem.at[it, n], (row_at(d, 0, 0), col))
-        if not it:
-            for d in reversed(ls):
-                send(mine_c, mine_c, 1, agl_sem.at[d - 1], (row, col_at(0, d)))
-            for d in ys:
-                send(mine_c, mine_c, 2, agy_sem.at[it], (row, col_at(d, 0)))
+        for d in ys:
+            send(mine_c, mine_c, 2, agy_sem.at[it], (row, col_at(d, 0)))
         for dx, dc in plane:
             send(mine_r, mine_r, 3, agx_sem.at[it, 0], (row_at(0, dx, dc), col))
 
-    def col_forward(d):
-        got = chunk_col(0, col_from(0, d))
-        arrive(got, agl_sem.at[d - 1])
+    def col_forward(it, d):
+        got = chunk_col(it, col_from(0, d))
+        arrive(got, agl_sem.at[it, d - 1])
         for dy in ys:
-            send(got, got, 2, agy_sem.at[0], (row, col_at(dy, 0)))
+            send(got, got, 2, agy_sem.at[it], (row, col_at(dy, 0)))
 
     def to_plane(it, got, late):
         for dx, dc in plane:
@@ -221,8 +220,7 @@
             to_plane(it, got, 1)
 
     def col_done(it):
-        count = ncol - 1 if it else (ny - 1) * nzl
-        arrive(colbuf.at[it, : 2 * count], agy_sem.at[it])
+        arrive(colbuf.at[it, : 2 * (ny - 1) * nzl], agy_sem.at[it])
 
     def near_done(it):
         arrive(rowbuf.at[it, : 2 * len(plane) * len(inner)], agx_sem.at[it, 0])
@@ -289,13 +287,38 @@
     def lower(it):
         terms(rows_s, rowsplit, 0)
         colterm[it] = product(hcol[...])
-        for n, (dy, dl) in enumerate(ring):
+        if DIRECT[it]:
+            for n, (dy, dl) in enumerate(ring):
+                send(
+                    colterm.at[it, pl.ds(2 * col_at(dy, dl), 2)],
+                    yrecv.at[it, n],
+                    5,
+                    rcy_sem.at[it, 0],
+                    (row, col_at(dy, dl)),
+                )
+            return
+        for dl in [*ls, 0]:
+            for n, dy in enumerate(ys):
+                send(
+                    colterm.at[it, pl.ds(2 * col_at(dy, dl), 2)],
+                    yrecv.at[it, dl * len(ys) + n],
+                    5,
+                    rcy_sem.at[it, 1 if dl else 2],
+                    (row, col_at(dy, 0)),
+                )
+
+    def col_reduce(it):
+        if DIRECT[it]:
+            return
+        count = len(ys)
+        arrive(yrecv.at[it, count : count * nzl], rcy_sem.at[it, 1])
+        for dl in ls:
+            total = colterm[it, pl.ds(2 * col_at(0, dl), 2)]
+            for n in range(count):
+                total = total + yrecv[it, dl * count + n]
+            lsend[it, dl - 1] = total
             send(
-                colterm.at[it, pl.ds(2 * col_at(dy, dl), 2)],
-                yrecv.at[it, n],
-                5,
-                rcy_sem.at[it],
-                (row, col_at(dy, dl)),
+                lsend.at[it, dl - 1], lrecv.at[it, dl - 1], 6, rcl_sem.at[it], (row, col_at(0, dl))
             )
 
     def plane_sum(it, dz):
@@ -315,10 +338,18 @@
         return total
 
     def col_final(it):
-        arrive(yrecv.at[it], rcy_sem.at[it])
         total = colterm[it, pl.ds(2 * col, 2)]
-        for n in range(ncol - 1):
+        if DIRECT[it]:
+            arrive(yrecv.at[it], rcy_sem.at[it, 0])
+            for n in range(ncol - 1):
+                total = total + yrecv[it, n]
+            return total
+        arrive(yrecv.at[it, : len(ys)], rcy_sem.at[it, 2])
+        for n in range(len(ys)):
             total = total + yrecv[it, n]
+        arrive(lrecv.at[it], rcl_sem.at[it])
+        for n in range(nzl - 1):
+            total = total + lrecv[it, n]
         return total
 
     lane = lax.broadcasted_iota(jnp.int32, (NRHS, TILE), 1)
@@ -414,14 +445,14 @@
 
     start_gather(0)
     for d in ls:
-        col_forward(d)
+        col_forward(0, d)
     near_arrive(0)
     near_forward(0)
     col_done(0)
     upper(0)
     to_rows(0, outer)
+    to_rows(0, inner)
     far_forward(0)
-    to_rows(0, inner)
     near_done(0)
     split_plane(0, inner)
     quad = jnp.zeros((NRHS, TILE), F32)
@@ -443,6 +474,7 @@
     row_done(0)
     split_plane(0, outer)
     lower(0)
+    col_reduce(0)
     red_send(0, 1, red_get(0, 0))
     total = row_final(0) + col_final(0)
     w = [
@@ -454,13 +486,15 @@
     put_masked(1, masked_w)
     start_gather(1)
     diag_w = own_terms(masked_w)
+    for d in ls:
+        col_forward(1, d)
     near_arrive(1)
     near_forward(1)
     col_done(1)
     upper(1)
     to_rows(1, outer)
+    to_rows(1, inner)
     far_forward(1)
-    to_rows(1, inner)
     near_done(1)
     split_plane(1, inner)
     first = red_get(0, 1)
@@ -495,6 +529,7 @@
     split_plane(1, outer)
     lower(1)
     red_send(2, 1, red_get(2, 0))
+    col_reduce(1)
     total = row_final(1) + col_final(1)
     second = red_get(1, 1)
     rr1, rw1 = unpack(second, 0), unpack(second, 1)
@@ -510,17 +545,19 @@
         here = slice(k * TILE, (k + 1) * TILE)
         direction = res[k] + beta * right[k]
         image = (w[k] - alpha * u[k]) + beta * w[k]
-        sol_ref[:, here] = alpha * right[k] + alpha1 * direction
-        res_ref[:, here] = res[k] - alpha1 * image
+        out_ref[0, :, here] = alpha * right[k] + alpha1 * direction
+        out_ref[1, :, here] = res[k] - alpha1 * image
 
     hops = 2 * (nzh - 1)
     sent(rowbuf.at[0, : 2 * hops], 0)
-    sent(rowbuf.at[0, : 2 * len(ls)], 1)
-    sent(rowbuf.at[0, : 2 * ((ny - 1) * nzl + ncol - 1)], 2)
+    sent(rowbuf.at[0, : 4 * len(ls)], 1)
+    sent(rowbuf.at[:, : 2 * (ny - 1) * nzl], 2)
     sent(rowbuf.at[:, : 2 * len(plane) * nzh], 3)
     sent(rowbuf.at[:, : 2 * len(plane) * nzh], 4)
-    sent(rowbuf.at[0, : 4 * (ncol - 1)], 5)
-    sent(rowbuf.at[0, : 2 * hops], 6)
+    counts = [ncol - 1 if DIRECT[it] else (ny - 1) * nzl for it in range(2)]
+    sent(rowbuf.at[0, : 2 * sum(counts)], 5)
+    extra = sum(0 if DIRECT[it] else nzl - 1 for it in range(2))
+    sent(rowbuf.at[0, : 2 * (hops + extra)], 6)
     sent(red_dst, 7)
 
 
@@ -545,12 +582,12 @@
     hbm = pl.BlockSpec(memory_space=pltpu.HBM)
     dma = pltpu.SemaphoreType.DMA
     chunk = (2, NRHS, TILE)
-    shape = jax.ShapeDtypeStruct(right_sides.shape, F32)
-    return pl.pallas_call(
+    shape = jax.ShapeDtypeStruct((2, *right_sides.shape), F32)
+    out = pl.pallas_call(
         functools.partial(kernel, rparts, cparts),
-        out_shape=(shape, shape),
+        out_shape=shape,
         in_specs=[hbm] * 8,
-        out_specs=(vmem, vmem),
+        out_specs=vmem,
         scratch_shapes=[
             pltpu.VMEM(right_sides.shape, F32),
             pltpu.VMEM((1, 2 * TILE), F32),
@@ -574,16 +611,19 @@
             pltpu.VMEM((2, nzh, *chunk), F32),
             pltpu.VMEM((2, nzh - 1, *chunk), F32),
             pltpu.VMEM((2, ncol - 1, *chunk), F32),
+            pltpu.VMEM((2, nzl - 1, *chunk), F32),
+            pltpu.VMEM((2, nzl - 1, *chunk), F32),
             pltpu.VMEM((3, 2, 1, TILE), F32),
             pltpu.VMEM((3, (plane + 1) * ny - 1 + nzh * nzl - 1, 1, TILE), F32),
             dma((8,)),
             dma((8,)),
             dma((2, 3)),
             dma((2, 2)),
-            dma((nzl - 1,)),
+            dma((2, nzl - 1)),
             dma((2,)),
             dma((2, nzh)),
             dma((2,)),
+            dma((2, 3)),
             dma((2,)),
             dma((3, 2)),
         ],
@@ -601,6 +641,7 @@
         tile_cols.reshape(slots),
         tile_count,
     )
+    return out[0], out[1]
 
 
 def solution(mesh):

time: 65.8 us -> 61.1 us (0.929)
  Pallas kernels: 62.4 us -> 58.3 us
    pallas_call x1, Pallas kernels: 62.4 us -> 58.3 us  [local(): pl.pallas_call(functools.partial(kernel, rparts, cparts), out_shape=shape...]
    unnamed x4 -> x0, local copies, waits for them, and re-layouts: 1.9 us -> none
    squeeze x0 -> x1, local copies, waits for them, and re-layouts: none -> 1.32 us  [local(): return (out[0], out[1])]
where the time goes in v5:
time: 61.1 us; the launch traced here: 60.9 us
  Pallas kernels  58.3 us (95%)
  local copies, waits for them, and re-layouts  1.32 us (2%)
  between operations  1.29 us (2%)
    pallas_call x1, Pallas kernels, local(): pl.pallas_call(functools.partial(kernel, rparts, cparts), out_shape=shape...  58.3 us
    squeeze x1, local copies, waits for them, and re-layouts, local(): return (out[0], out[1])  1.32 us

profile of v5, /device:TPU:1, one launch (start us, length us, event | category | flops | bytes accessed | tf_op | source)
XLA Modules:
  0.0 60.9 jit_solution(15355488227894016929)
XLA Ops:
  1.3 58.3 %solve.1 = f32[2,8,256]{2,1,0:T(8,128)} custom-call(f32[8,256]{1,0:T(8,128)} %rs_hbm.1, f32[1,256]{1,0:T(1,128)} %bitcast.10, s32[1,256]{1,0:T(1,128)} %bitcast.11, bf16[2,128,128]{2,1,0:T(8,128)(2,1)} %diag_hbm.1, bf16[32,128,128]{2,1,0:T(8,128)(2,1)} %bitcast.9, s32[32]{0:T(128)} %bitcast.12, s32[32]{0:T(128)} %bitcast.13, s32[1,1]{1,0:T(1,128)S(6)} %copy.10.count_hbm), custom_call_target="tpu_custom_call" | custom-call | tf_op jit(solution)/shard_map/solve/pallas_call | solution.py:586
  59.6 1.3 %slice_bitcast_fusion = (f32[8,256]{1,0:T(8,128)}, f32[8,256]{1,0:T(8,128)}) fusion(f32[2,8,256]{2,1,0:T(8,128)} %solve.1), kind=kLoop, calls=%fused_computation | loop fusion | bytes 32768 | tf_op jit(solution)/shard_map/squeeze | solution.py:644
